TPU v7x, 256 devices: a whole 4x4x8 slice. The times are simulated.
256 devices in a mesh: slab: 128 (over y, x, z_hi, core), grp: 2 (over z_lo).
Axes of the slice: x: 4, y: 4, z: 8 (z_hi: 4, z_lo: 2; z = z_hi * 2 + z_lo), core: 2. Of those that a mesh axis runs over, the one named last changes fastest.
Arguments:
- saturation: float32 [256, 64, 256], P(('slab', 'grp')), may hold values from 0.5 to 3
- inlet_mask: int32 [256, 64, 256], P(('slab', 'grp')), may hold values 0 or 1
- crystal_size: float32 [1048576], P(('slab', 'grp')), may hold values from 0.5 to 2
- crystal_weight: float32 [1048576], P(('slab', 'grp')), may hold values from 0.3 to 3
- crystal_cell: int32 [1048576], P(('slab', 'grp')), may hold values from 0 to 32767
- live_count: int32 [256], P(('slab', 'grp')), may hold values from 1024 to 4096, as said below
- nucleus_cell: int32 [256, 4, 512], P(('slab', 'grp')), may hold values from 0 to 32767
- nucleus_count: int32 [256, 4, 512], P(('slab', 'grp')), may hold values from 1 to 8
- migrant_rows: int32 [256, 2, 512], P(('slab', 'grp')), may hold values from 0 to 4095, as said below
- migrant_count: int32 [256, 2], P(('slab', 'grp')), may hold values from 0 to 512
Outputs:
- saturation_out: float32 [256, 64, 256], P(('slab', 'grp'))
- size_out: float32 [1048576], P(('slab', 'grp'))
- arrivals: float32 [256, 2, 2, 512], P(('slab', 'grp'))
Inputs may be any that keep to these rules, and one draw needn't show every extreme that they name: `live_count`: about a quarter of the devices hold exactly 4096 live rows, the others a quarter to a third of that. `migrant_rows`: rows of the device's own parcels below its live count, all distinct; the list toward the lower slab lies in the lower half of the live rows, the other in the upper half.
All inputs are finite; a program needn't handle non-finite values. No bound on the sum of `inlet_mask` on one device may be relied on, other than what follows from the above.
Results may differ from a plain program's by a relative error of at most 0.00007.
Values sent between devices are 32-bit elements; how exact they have to be, the bound alone decides.
A program may use at most 64 MiB of HBM per device.

v0:
```python
import jax
import jax.numpy as jnp
from jax import lax
from jax.sharding import PartitionSpec as P

BLOCK = 2048
STEPS = 2
SUBS = 2


GROWTH = 0.08
VOLUME = 1.0
NUCLEATE = 0.02
DIFFUSE = 0.12
INLET = 4.0


def extended(cells, sides, width):
    for axis, dim in sides:
        count = lax.axis_size(axis)
        ends = count - 1
        head = lax.slice_in_dim(cells, 0, width, axis=dim)
        tail = lax.slice_in_dim(cells, cells.shape[dim] - width, cells.shape[dim], axis=dim)
        cells = jnp.concatenate(
            [
                lax.ppermute(tail, axis, [(i, (i + 1) % count) for i in range(ends)]),
                cells,
                lax.ppermute(head, axis, [((i + 1) % count, i) for i in range(ends)]),
            ],
            axis=dim,
        )
    return cells


def passed_along(value, axis, steps):
    count = lax.axis_size(axis)
    leading, last = (max(0, -steps), min(count, count - steps))
    return lax.ppermute(value, axis, [(source, source + steps) for source in range(leading, last)])


def transport(padded_x, inlet_weight):
    field_mid = padded_x[1:-1]
    padded_yz = jnp.pad(field_mid, ((0, 0), (1, 1), (1, 1)))
    beside = padded_x[2:] + padded_x[:-2]
    beside = beside + padded_yz[:, 2:, 1:-1] + padded_yz[:, :-2, 1:-1]
    beside = beside + padded_yz[:, 1:-1, 2:] + padded_yz[:, 1:-1, :-2]
    field_mid = field_mid + DIFFUSE * (beside - 6.0 * field_mid)
    return field_mid + inlet_weight * (INLET - field_mid)


def cell_tables(cells, line_count, line_width):
    line_of = cells // line_width
    place_of = cells % line_width
    hot_line = (line_of[:, None] == lax.iota(jnp.int32, line_count)[None, :]).astype(jnp.float32)
    hot_place = (place_of[:, None] == lax.iota(jnp.int32, line_width)[None, :]).astype(jnp.float32)
    return (hot_line, hot_place)


def read_cells(slab_lines, hot_line, hot_place):
    picked = jnp.dot(
        hot_line, slab_lines, precision=lax.Precision.HIGHEST, preferred_element_type=jnp.float32
    )
    return jnp.sum(picked * hot_place, axis=1)


def spread_cells(hot_line, hot_place, mass):
    return lax.dot_general(
        hot_line,
        hot_place * mass[:, None],
        (((0,), (0,)), ((), ())),
        precision=lax.Precision.HIGHEST,
        preferred_element_type=jnp.float32,
    )


def parcel_step(
    slab_lines, crystal, crystal_weight, crystal_cell, live_total, event_cell, event_count
):
    line_count, line_width = slab_lines.shape
    parcels = crystal.shape[0]
    event_line, event_place = cell_tables(event_cell, line_count, line_width)
    event_mass = (
        event_count.astype(jnp.float32)
        * NUCLEATE
        * jax.nn.softplus(read_cells(slab_lines, event_line, event_place) - 1.0)
    )
    deposit = spread_cells(event_line, event_place, event_mass)

    def one_block(block_index, state_pair):
        sizes_now, deposit_now = state_pair
        first_row = block_index * BLOCK
        part_size = lax.dynamic_slice_in_dim(sizes_now, first_row, BLOCK)
        part_weight = lax.dynamic_slice_in_dim(crystal_weight, first_row, BLOCK)
        part_cell = lax.dynamic_slice_in_dim(crystal_cell, first_row, BLOCK)
        part_live = (first_row + lax.iota(jnp.int32, BLOCK) < live_total).astype(jnp.float32)
        hot_line, hot_place = cell_tables(part_cell, line_count, line_width)
        local_sat = read_cells(slab_lines, hot_line, hot_place)
        enlarged = part_size + part_live * GROWTH * jax.nn.softplus(local_sat - 1.0)
        consumed = (
            part_live
            * part_weight
            * VOLUME
            * (enlarged * enlarged * enlarged - part_size * part_size * part_size)
        )
        sizes_now = lax.dynamic_update_slice_in_dim(sizes_now, enlarged, first_row, 0)
        return (sizes_now, deposit_now + spread_cells(hot_line, hot_place, consumed))

    block_count = parcels // BLOCK
    crystal, deposit = lax.fori_loop(0, block_count, one_block, (crystal, deposit))
    return (crystal, deposit)


def local(
    saturation,
    inlet_mask,
    crystal_size,
    crystal_weight,
    crystal_cell,
    live_count,
    nucleus_cell,
    nucleus_count,
    migrant_rows,
    migrant_count,
):
    width_z = saturation.shape[2]
    parcels = crystal_size.shape[0]
    slots = migrant_rows.shape[2]
    live_total = live_count[0]
    active_rows = (lax.iota(jnp.int32, parcels) < live_total).astype(jnp.float32)
    inlet_weight = inlet_mask.astype(jnp.float32)
    crystal = crystal_size
    field = saturation
    for step_index in range(STEPS):
        for sub_index in range(SUBS):
            substep = step_index * SUBS + sub_index
            slab_field = lax.all_gather(field, "grp", axis=0, tiled=True)
            crystal, deposit = parcel_step(
                slab_field.reshape(-1, width_z),
                crystal,
                crystal_weight,
                crystal_cell,
                live_total,
                nucleus_cell[0, substep],
                nucleus_count[0, substep],
            )
            field = field - lax.psum_scatter(
                deposit.reshape(slab_field.shape), "grp", scatter_dimension=0, tiled=True
            )
        padded_x = extended(field, ((("slab", "grp"), 0),), 1)
        field = transport(padded_x, inlet_weight)
    size_out = active_rows * crystal
    rows = migrant_rows[0]
    slot_live = (lax.iota(jnp.int32, slots)[None, :] < migrant_count[0][:, None]).astype(
        jnp.float32
    )
    sent = (
        jnp.stack([jnp.take(size_out, rows), jnp.take(crystal_weight, rows)], axis=1)
        * slot_live[:, None, :]
    )
    from_lower = passed_along(sent[1], "slab", 1)
    from_upper = passed_along(sent[0], "slab", -1)
    arrivals = jnp.stack([from_lower, from_upper], axis=0)[None]
    return (field, size_out, arrivals)


def solution(mesh):
    in_specs = (
        P(("slab", "grp"), None, None),
        P(("slab", "grp"), None, None),
        P(("slab", "grp")),
        P(("slab", "grp")),
        P(("slab", "grp")),
        P(("slab", "grp")),
        P(("slab", "grp"), None, None),
        P(("slab", "grp"), None, None),
        P(("slab", "grp"), None, None),
        P(("slab", "grp"), None),
    )
    out_specs = (
        P(("slab", "grp"), None, None),
        P(("slab", "grp")),
        P(("slab", "grp"), None, None, None),
    )
    return jax.shard_map(local, mesh=mesh, in_specs=in_specs, out_specs=out_specs, check_vma=False)
```

profile of v0, /device:TPU:24, one launch (start us, length us, event | category | flops | bytes accessed | tf_op | source)
XLA Modules:
  0.0 174.3 jit_solution(10607794521240898568)
XLA Ops:
  8.1 5.1 %all_gather.12 = f32[2,64,256]{2,1,0:T(8,128)S(1)} all-gather(f32[1,64,256]{2,1,0:T(8,128)} %param.20), channel_id=1, replica_groups=mesh['slab'=128,'grp'=2] {'grp'}, dimensions={0}, use_global_device_ids=true | all-gather | bytes 196608 | tf_op jit(solution)/shard_map/all_gather | solution.py:136
  14.6 8.8 %while.68 = (s32[]{:T(128)}, f32[4096]{0:T(1024)S(1)}, f32[128,256]{1,0:T(8,128)S(1)}, s32[]{:T(128)}, s32[4096]{0:T(1024)S(1)}, /*index=5*/f32[128,256]{1,0:T(8...) while((s32[]{:T(128)}, f32[4096]{0:T(1024)S(1)}, ...), condition=%wide.region_3.4_spmd, body=%wide.region_1.3_spmd.sunk | while | flops 1614141440 | bytes 536763 | solution.py:109
  17.3 1.7 fusion.186
  24.2 18.3 %reduce-scatter.5.cloned.1.call-done = f32[1,64,256]{2,1,0:T(8,128)} async-done(((f32[2,64,256]{2,1,0:T(8,128)}), f32[1,64,256]{2,1,0:T(8,128)}) %reduce-scatter.5.cloned.1.call-update) | async-done | bytes 65552 | tf_op jit(solution)/shard_map/reduce_scatter | solution.py:146
  43.3 4.9 %all_gather.13 = f32[2,64,256]{2,1,0:T(8,128)S(1)} all-gather(f32[1,64,256]{2,1,0:T(8,128)S(1)} %sub.150), channel_id=1, replica_groups=mesh['slab'=128,'grp'=2] {'grp'}, dimensions={0}, use_global_device_ids=true | all-gather | bytes 196608 | tf_op jit(solution)/shard_map/all_gather | solution.py:136
  49.3 8.8 %while.69 = (s32[]{:T(128)}, f32[4096]{0:T(1024)S(1)}, f32[128,256]{1,0:T(8,128)S(1)}, s32[]{:T(128)}, s32[4096]{0:T(1024)S(1)}, /*index=5*/f32[128,256]{1,0:T(8...) while((s32[]{:T(128)}, f32[4096]{0:T(1024)S(1)}, ...), condition=%wide.region_8.9_spmd, body=%wide.region_6.8_spmd.sunk | while | flops 1614141440 | bytes 536763 | solution.py:109
  59.0 16.0 %reduce-scatter.7.cloned.1.call-done = f32[1,64,256]{2,1,0:T(8,128)} async-done(((f32[2,64,256]{2,1,0:T(8,128)}), f32[1,64,256]{2,1,0:T(8,128)}) %reduce-scatter.7.cloned.1.call-update) | async-done | bytes 65552 | tf_op jit(solution)/shard_map/reduce_scatter | solution.py:146
  75.8 6.7 %collective-permute-start = (f32[1,64,256]{2,1,0:T(8,128)S(1)}, f32[1,64,256]{2,1,0:T(8,128)S(1)}, u32[]{:S(2)}, u32[]{:S(2)}) collective-permute-start(f32[1,64,256]{2,1,0:T(8,128)S(1)} %sub.153), channel_id=1, source_target_pairs={{1,0},{2,1},{3,2},{4,3},{5,4},{6,5},{7,6},{8,7},{9,8},{10,9},{11,1... | collective-permute-start | bytes 196616 | tf_op jit(solution)/shard_map/ppermute | solution.py:28
  82.4 1.9 %collective-permute-start.1 = (f32[1,64,256]{2,1,0:T(8,128)S(1)}, f32[1,64,256]{2,1,0:T(8,128)S(1)}, u32[]{:S(2)}, u32[]{:S(2)}) collective-permute-start(f32[1,64,256]{2,1,0:T(8,128)S(1)} %sub.153), channel_id=1, source_target_pairs={{0,1},{1,2},{2,3},{3,4},{4,5},{5,6},{6,7},{7,8},{8,9},{9,10},{10,1... | collective-permute-start | bytes 196616 | tf_op jit(solution)/shard_map/ppermute | solution.py:26
  84.4 7.8 %collective-permute-done.1 = f32[1,64,256]{2,1,0:T(8,128)S(1)} collective-permute-done((f32[1,64,256]{2,1,0:T(8,128)S(1)}, f32[1,64,256]{2,1,0:T(8,128)S(1)}, u32[]{:S(2)}, u32[]{:S(2)}) %collective-permute-start.1) | collective-permute-done | bytes 65568 | tf_op jit(solution)/shard_map/ppermute | solution.py:26
  92.3 4.9 %all_gather.14 = f32[2,64,256]{2,1,0:T(8,128)S(1)} all-gather(f32[1,64,256]{2,1,0:T(8,128)S(1)} %multiply_add_fusion.1), channel_id=1, replica_groups=mesh['slab'=128,'grp'=2] {'grp'}, dimensions={0}, use_global_device_ids=true | all-gather | bytes 196608 | tf_op jit(solution)/shard_map/all_gather | solution.py:136
  98.3 8.8 %while.70 = (s32[]{:T(128)}, f32[4096]{0:T(1024)S(1)}, f32[128,256]{1,0:T(8,128)S(1)}, s32[]{:T(128)}, s32[4096]{0:T(1024)S(1)}, /*index=5*/f32[128,256]{1,0:T(8...) while((s32[]{:T(128)}, f32[4096]{0:T(1024)S(1)}, ...), condition=%wide.region_13.14_spmd, body=%wide.region_11.13_spmd.sunk | while | flops 1614141440 | bytes 536763 | solution.py:109
  101.1 1.7 fusion.198
  108.7 6.2 %gather_fusion.1 = f32[1024]{0:T(1024)S(1)} fusion(f32[4096]{0:T(1024)S(1)} %get-tuple-element.1170, s32[1024]{0:T(1024)S(1)} %broadcast_clamp_fusion), kind=kCustom, calls=%fused_computation.1.clone | custom fusion | bytes 12288 | tf_op jit(solution)/shard_map/jit(_take)/gather | solution.py:157
  114.8 2.1 %reduce-scatter.9.cloned.1.call-done = f32[1,64,256]{2,1,0:T(8,128)} async-done(((f32[2,64,256]{2,1,0:T(8,128)}), f32[1,64,256]{2,1,0:T(8,128)}) %reduce-scatter.9.cloned.1.call-update) | async-done | bytes 65552 | tf_op jit(solution)/shard_map/reduce_scatter | solution.py:146
  117.8 5.1 %all_gather.15 = f32[2,64,256]{2,1,0:T(8,128)S(1)} all-gather(f32[1,64,256]{2,1,0:T(8,128)S(1)} %sub.158), channel_id=1, replica_groups=mesh['slab'=128,'grp'=2] {'grp'}, dimensions={0}, use_global_device_ids=true | all-gather | bytes 196608 | tf_op jit(solution)/shard_map/all_gather | solution.py:136
  124.0 8.8 %while.71 = (s32[]{:T(128)}, f32[4096]{0:T(1024)S(1)}, f32[128,256]{1,0:T(8,128)S(1)}, s32[]{:T(128)}, s32[4096]{0:T(1024)S(1)}, /*index=5*/f32[128,256]{1,0:T(8...) while((s32[]{:T(128)}, f32[4096]{0:T(1024)S(1)}, ...), condition=%wide.region_18.19_spmd, body=%wide.region_16.18_spmd.sunk | while | flops 1614141440 | bytes 536763 | solution.py:109
  133.6 6.2 %gather_fusion = f32[1024]{0:T(1024)S(1)} fusion(f32[4096]{0:T(1024)S(1)} %fusion.130, s32[1024]{0:T(1024)S(1)} %broadcast_clamp_fusion), kind=kCustom, calls=%fused_computation.clone | custom fusion | bytes 12288 | tf_op jit(solution)/shard_map/jit(_take)/gather | solution.py:157
  139.8 5.6 %collective-permute-start.5 = (f32[2,512]{1,0:T(2,128)S(1)}, f32[2,512]{1,0:T(2,128)S(1)}, u32[]{:S(2)}, u32[]{:S(2)}) collective-permute-start(f32[2,512]{1,0:T(2,128)S(1)} %get-tuple-element.809), channel_id=1, source_target_pairs={{2,0},{4,2},{6,4},{8,6},{10,8},{12,10},{14,12},{16,14},{18,16},{20... | collective-permute-start | bytes 12296 | tf_op jit(solution)/shard_map/ppermute | solution.py:38
  145.4 1.9 %collective-permute-start.4 = (f32[2,512]{1,0:T(2,128)S(1)}, f32[2,512]{1,0:T(2,128)S(1)}, u32[]{:S(2)}, u32[]{:S(2)}) collective-permute-start(f32[2,512]{1,0:T(2,128)S(1)} %get-tuple-element.808), channel_id=1, source_target_pairs={{0,2},{2,4},{4,6},{6,8},{8,10},{10,12},{12,14},{14,16},{16,18},{18... | collective-permute-start | bytes 12296 | tf_op jit(solution)/shard_map/ppermute | solution.py:38
  147.3 2.3 %reduce-scatter.11.cloned.1.call-done = f32[1,64,256]{2,1,0:T(8,128)} async-done(((f32[2,64,256]{2,1,0:T(8,128)}), f32[1,64,256]{2,1,0:T(8,128)}) %reduce-scatter.11.cloned.1.call-update) | async-done | bytes 65552 | tf_op jit(solution)/shard_map/reduce_scatter | solution.py:146
  150.5 6.7 %collective-permute-start.2 = (f32[1,64,256]{2,1,0:T(8,128)S(1)}, f32[1,64,256]{2,1,0:T(8,128)S(1)}, u32[]{:S(2)}, u32[]{:S(2)}) collective-permute-start(f32[1,64,256]{2,1,0:T(8,128)S(1)} %sub.161), channel_id=1, source_target_pairs={{1,0},{2,1},{3,2},{4,3},{5,4},{6,5},{7,6},{8,7},{9,8},{10,9},{11,1... | collective-permute-start | bytes 196616 | tf_op jit(solution)/shard_map/ppermute | solution.py:28
  157.2 1.9 %collective-permute-start.3 = (f32[1,64,256]{2,1,0:T(8,128)S(1)}, f32[1,64,256]{2,1,0:T(8,128)S(1)}, u32[]{:S(2)}, u32[]{:S(2)}) collective-permute-start(f32[1,64,256]{2,1,0:T(8,128)S(1)} %sub.161), channel_id=1, source_target_pairs={{0,1},{1,2},{2,3},{3,4},{4,5},{5,6},{6,7},{7,8},{8,9},{9,10},{10,1... | collective-permute-start | bytes 196616 | tf_op jit(solution)/shard_map/ppermute | solution.py:26
  159.7 7.2 %collective-permute-done.3 = f32[1,64,256]{2,1,0:T(8,128)S(1)} collective-permute-done((f32[1,64,256]{2,1,0:T(8,128)S(1)}, f32[1,64,256]{2,1,0:T(8,128)S(1)}, u32[]{:S(2)}, u32[]{:S(2)}) %collective-permute-start.3) | collective-permute-done | bytes 65568 | tf_op jit(solution)/shard_map/ppermute | solution.py:26
  (121 shorter events, 44.6 us)
Async XLA Ops:
  7.2 6.1 %copy-start.11 = (s32[1,4,512]{2,1,0:T(4,128)S(1)}, s32[1,4,512]{2,1,0:T(4,128)}, u32[]{:S(2)}) copy-start(s32[1,4,512]{2,1,0:T(4,128)} %param.26) | copy-start | bytes 24580
  7.2 35.3 %reduce-scatter.5.cloned.1.call-start = ((), (), s32[]{:S(2)}) async-start(), calls=%async_computation.4 | async-start | bytes 196608 | tf_op jit(solution)/shard_map/reduce_scatter | solution.py:146
  13.8 0.7 copy-start
  13.8 0.7 copy-start.2
  13.8 0.7 copy-start.3
  23.4 0.7 copy-start.9
  23.4 19.1 %copy-start.4 = (f32[1,64,256]{2,1,0:T(8,128)S(1)}, f32[1,64,256]{2,1,0:T(8,128)}, u32[]{:S(2)}) copy-start(f32[1,64,256]{2,1,0:T(8,128)} %param.20) | copy-start | bytes 196612
  24.1 50.8 %reduce-scatter.7.cloned.1.call-start = ((), (), s32[]{:S(2)}) async-start(), calls=%async_computation.5 | async-start | bytes 196608 | tf_op jit(solution)/shard_map/reduce_scatter | solution.py:146
  58.2 0.7 copy-start.6
  58.2 0.7 copy-start.10
  58.9 33.4 %copy-start.5 = (s32[1,64,256]{2,1,0:T(8,128)S(1)}, s32[1,64,256]{2,1,0:T(8,128)}, u32[]{:S(2)}) copy-start(s32[1,64,256]{2,1,0:T(8,128)} %param.21) | copy-start | bytes 196612
  58.9 58.1 %reduce-scatter.9.cloned.1.call-start = ((), (), s32[]{:S(2)}) async-start(), calls=%async_computation.6 | async-start | bytes 196608 | tf_op jit(solution)/shard_map/reduce_scatter | solution.py:146
  75.8 8.6 %collective-permute-start = (f32[1,64,256]{2,1,0:T(8,128)S(1)}, f32[1,64,256]{2,1,0:T(8,128)S(1)}, u32[]{:S(2)}, u32[]{:S(2)}) collective-permute-start(f32[1,64,256]{2,1,0:T(8,128)S(1)} %sub.153), channel_id=1, source_target_pairs={{1,0},{2,1},{3,2},{4,3},{5,4},{6,5},{7,6},{8,7},{9,8},{10,9},{11,1... | collective-permute-start | bytes 196616 | tf_op jit(solution)/shard_map/ppermute | solution.py:28
  82.4 9.8 %collective-permute-start.1 = (f32[1,64,256]{2,1,0:T(8,128)S(1)}, f32[1,64,256]{2,1,0:T(8,128)S(1)}, u32[]{:S(2)}, u32[]{:S(2)}) collective-permute-start(f32[1,64,256]{2,1,0:T(8,128)S(1)} %sub.153), channel_id=1, source_target_pairs={{0,1},{1,2},{2,3},{3,4},{4,5},{5,6},{6,7},{7,8},{8,9},{9,10},{10,1... | collective-permute-start | bytes 196616 | tf_op jit(solution)/shard_map/ppermute | solution.py:26
  107.2 0.7 copy-start.7
  107.2 0.7 copy-start.12
  107.9 41.8 %reduce-scatter.11.cloned.1.call-start = ((), (), s32[]{:S(2)}) async-start(), calls=%async_computation.7 | async-start | bytes 196608 | tf_op jit(solution)/shard_map/reduce_scatter | solution.py:146
  132.9 0.7 copy-start.8
  133.6 6.2 %copy-start.1 = (f32[4096]{0:T(1024)}, f32[4096]{0:T(1024)S(1)}, u32[]{:S(2)}) copy-start(f32[4096]{0:T(1024)S(1)} %fusion.130) | copy-start | bytes 49156
  139.8 19.3 %collective-permute-start.5 = (f32[2,512]{1,0:T(2,128)S(1)}, f32[2,512]{1,0:T(2,128)S(1)}, u32[]{:S(2)}, u32[]{:S(2)}) collective-permute-start(f32[2,512]{1,0:T(2,128)S(1)} %get-tuple-element.809), channel_id=1, source_target_pairs={{2,0},{4,2},{6,4},{8,6},{10,8},{12,10},{14,12},{16,14},{18,16},{20... | collective-permute-start | bytes 12296 | tf_op jit(solution)/shard_map/ppermute | solution.py:38
  145.4 13.7 %collective-permute-start.4 = (f32[2,512]{1,0:T(2,128)S(1)}, f32[2,512]{1,0:T(2,128)S(1)}, u32[]{:S(2)}, u32[]{:S(2)}) collective-permute-start(f32[2,512]{1,0:T(2,128)S(1)} %get-tuple-element.808), channel_id=1, source_target_pairs={{0,2},{2,4},{4,6},{6,8},{8,10},{10,12},{12,14},{14,16},{16,18},{18... | collective-permute-start | bytes 12296 | tf_op jit(solution)/shard_map/ppermute | solution.py:38
  150.5 9.3 %collective-permute-start.2 = (f32[1,64,256]{2,1,0:T(8,128)S(1)}, f32[1,64,256]{2,1,0:T(8,128)S(1)}, u32[]{:S(2)}, u32[]{:S(2)}) collective-permute-start(f32[1,64,256]{2,1,0:T(8,128)S(1)} %sub.161), channel_id=1, source_target_pairs={{1,0},{2,1},{3,2},{4,3},{5,4},{6,5},{7,6},{8,7},{9,8},{10,9},{11,1... | collective-permute-start | bytes 196616 | tf_op jit(solution)/shard_map/ppermute | solution.py:28
  157.2 9.8 %collective-permute-start.3 = (f32[1,64,256]{2,1,0:T(8,128)S(1)}, f32[1,64,256]{2,1,0:T(8,128)S(1)}, u32[]{:S(2)}, u32[]{:S(2)}) collective-permute-start(f32[1,64,256]{2,1,0:T(8,128)S(1)} %sub.161), channel_id=1, source_target_pairs={{0,1},{1,2},{2,3},{3,4},{4,5},{5,6},{6,7},{7,8},{8,9},{9,10},{10,1... | collective-permute-start | bytes 196616 | tf_op jit(solution)/shard_map/ppermute | solution.py:26
Sparse Core Ops, SparseCore 0:
  24.2 18.2 reduce-scatter.4
  59.0 15.8 reduce-scatter.6
  108.0 8.9 reduce-scatter.8
  133.7 15.9 reduce-scatter.10
where the time goes:
time: 175 us; the launch traced here: 174 us
  waiting for transfers between devices  53.9 us (31%)
  matrix products  30.9 us (18%)
  starting transfers between devices  24.9 us (14%)
  blocking collectives  20.1 us (11%)
  local copies, waits for them, and re-layouts  17.7 us (10%)
  between operations  14.9 us (9%)
  other arithmetic  11.5 us (7%)
    reduce_scatter x4, waiting for transfers between devices, local(): lax.psum_scatter(deposit.reshape(slab_field.shape), 'grp', scatter_dimens...  38.7 us
    all_gather x4, blocking collectives, local(): slab_field = lax.all_gather(field, 'grp', axis=0, tiled=True)  20.1 us
    dot_general x12, matrix products, spread_cells(): lax.dot_general(hot_line, hot_place * mass[:, None], (((0,), (0,)), ((),...  15.5 us
    dot_general x12, matrix products, read_cells(): jnp.dot(hot_line, slab_lines, precision=lax.Precision.HIGHEST, preferred_...  15.4 us
    ppermute x2, waiting for transfers between devices, extended(): lax.ppermute(tail, axis, [(i, (i + 1) % count) for i in range(ends)])  15.1 us
    ppermute x2, starting transfers between devices, extended(): lax.ppermute(head, axis, [((i + 1) % count, i) for i in range(ends)])  13.3 us
    ppermute x2, starting transfers between devices, passed_along(): lax.ppermute(value, axis, [(source, source + steps) for source in range(l...  7.5 us
    gather x2, local copies, waits for them, and re-layouts, local(): jnp.take(crystal_weight, rows)  6.16 us
  transfers between devices with their start and end apart: 10, of which 6 were waited for; matrix products, arithmetic and copies ran while one was open for 8% of the time, Pallas kernels for 0%

commit v1 on v0

v1 whole, which is shorter than its diff:
```python
import jax
import jax.numpy as jnp
from jax import lax
from jax.experimental import pallas as pl
from jax.experimental.pallas import tpu as pltpu
from jax.sharding import PartitionSpec as P

STEPS = 2
SUBS = 2
GROWTH = 0.08
VOLUME = 1.0
NUCLEATE = 0.02
DIFFUSE = 0.12
INLET = 4.0

LANES = 128
ROWS = 8
CHUNK = ROWS * LANES
MESH = pl.DeviceIdType.MESH
F32 = jnp.float32
BF16 = jnp.bfloat16
I32 = jnp.int32


def softplus(x):
    return jnp.maximum(x, 0.0) + jnp.log1p(jnp.exp(-jnp.abs(x)))


def pieces(x, count):
    out = []
    for _ in range(count):
        top = x.astype(BF16)
        out.append(top)
        x = x - top.astype(F32)
    return out


def kernel(
    live_ref,
    mcount_ref,
    sat_hbm,
    inlet_hbm,
    size_hbm,
    weight_hbm,
    cell_hbm,
    ncell_hbm,
    ncount_hbm,
    mrows_hbm,
    field_ref,
    size_ref,
    arrive_ref,
    field,
    inlet,
    sizes,
    weights,
    cells,
    cells_in,
    ncell,
    ncount,
    mrows,
    evcell,
    evcount,
    halo,
    back,
    mig_out,
    mig_in,
    plane_out,
    size_send,
    hot_p,
    hot_t,
    hot_l,
    pair,
    local,
    mass_hi,
    mass_lo,
    mig_hot,
    mig_line,
    local_sem,
    send_sem,
    recv_sem,
):
    ny, nz = field.shape
    plane_cells = ny * nz
    shift = nz.bit_length() - 1
    half = sizes.shape[0] // 2
    parcel_chunks = 2 * half
    s = lax.axis_index("slab")
    g = lax.axis_index("grp")
    slabs = lax.axis_size("slab")
    up = (lax.rem(s + 1, slabs), g)
    down = (lax.rem(s + slabs - 1, slabs), g)
    partner = (s, 1 - g)
    other = (lax.rem(s + slabs + 2 * g - 1, slabs), 1 - g)

    barrier = pltpu.get_barrier_semaphore()
    for peer in (partner, other, up, down):
        pl.semaphore_signal(barrier, inc=1, device_id=peer, device_id_type=MESH)

    loads = []
    for index, (source, target) in enumerate(
        (
            (cell_hbm, cells_in),
            (sat_hbm.at[0], field),
            (size_hbm, sizes.at[pl.ds(0, half)]),
            (weight_hbm, weights.at[pl.ds(0, half)]),
            (ncell_hbm.at[0], ncell.at[0]),
            (ncount_hbm.at[0], ncount.at[0]),
            (inlet_hbm.at[0], inlet),
            (mrows_hbm.at[0], mrows),
        )
    ):
        copy = pltpu.make_async_copy(source, target, local_sem.at[index])
        copy.start()
        loads.append(copy)

    def remote(index, source, target, peer):
        copy = pltpu.make_async_remote_copy(
            src_ref=source,
            dst_ref=target,
            send_sem=send_sem.at[index],
            recv_sem=recv_sem.at[index],
            device_id=peer,
            device_id_type=MESH,
        )
        copy.start()
        return copy

    loads[0].wait()
    live = live_ref[0]
    row_of = (
        lax.broadcasted_iota(I32, (half, ROWS, LANES), 0) * CHUNK
        + lax.broadcasted_iota(I32, (half, ROWS, LANES), 1) * LANES
        + lax.broadcasted_iota(I32, (half, ROWS, LANES), 2)
    )
    is_live = row_of < live
    cells_in[...] = jnp.where(is_live, cells_in[...], -1)
    cells[pl.ds(0, half)] = cells_in[...]

    pl.semaphore_wait(barrier, 4)
    entry = [
        remote(0, cells_in, cells.at[pl.ds(half, half)], partner),
        remote(1, size_hbm, sizes.at[pl.ds(half, half)], partner),
        remote(2, weight_hbm, weights.at[pl.ds(half, half)], partner),
        remote(3, ncell_hbm.at[0], ncell.at[1], partner),
        remote(4, ncount_hbm.at[0], ncount.at[1], partner),
    ]

    base = g * plane_cells
    down_nz = lax.broadcasted_iota(I32, (nz, LANES), 0)
    down_ny = lax.broadcasted_iota(I32, (ny, LANES), 0)
    along_nz = lax.broadcasted_iota(I32, (LANES, nz), 1)

    def build(chunk, tile):
        cell = tile - base
        place = cell & (nz - 1)
        line = cell >> shift
        turned = jnp.transpose(place)
        for j in range(ROWS):
            columns = pl.ds(LANES * j, LANES)
            hot_p[chunk, :, columns] = jnp.where(
                down_nz == place[j : j + 1, :], 1.0, 0.0
            ).astype(BF16)
            hot_l[chunk, :, columns] = jnp.where(
                down_ny == line[j : j + 1, :], 1.0, 0.0
            ).astype(BF16)
            hot_t[chunk, columns, :] = jnp.where(
                along_nz == jnp.broadcast_to(turned[:, j : j + 1], (LANES, nz)),
                1.0,
                0.0,
            ).astype(BF16)

    def build_parcels(first, last):
        def body(chunk, carry):
            build(chunk, cells[chunk])
            return carry

        lax.fori_loop(first, last, body, 0)

    def build_events(sub):
        rows = ROWS // 2
        for side in range(2):
            for j in range(rows):
                columns = pl.ds(LANES * j, LANES)
                at = pl.ds(side * rows + j, 1)
                evcell[sub, at, :] = ncell[side, pl.ds(sub, 1), columns]
                evcount[sub, at, :] = ncount[side, pl.ds(sub, 1), columns].astype(F32)
        build(parcel_chunks + sub, evcell[sub])

    def split_field():
        top, rest = pieces(field[...], 2)
        pair[pl.ds(0, ny), :] = top
        pair[pl.ds(ny, ny), :] = rest

    def gather(chunk):
        both = jnp.dot(pair[...], hot_p[chunk], preferred_element_type=F32)
        read = (both[:ny] + both[ny:]) * hot_l[chunk].astype(F32)
        flat = jnp.sum(read, axis=0, keepdims=True)
        for j in range(ROWS):
            local[chunk, pl.ds(j, 1), :] = flat[:, LANES * j : LANES * (j + 1)]

    def set_mass(chunk, mass):
        top = mass.astype(BF16).astype(F32)
        mass_hi[chunk] = top
        mass_lo[chunk] = mass - top

    def grow(chunk):
        line = (cells[chunk] - base) >> shift
        here = jnp.where((line >= 0) & (line < ny), 1.0, 0.0)
        size = sizes[chunk]
        grown = size + here * GROWTH * softplus(local[chunk] - 1.0)
        sizes[chunk] = grown
        set_mass(
            chunk,
            here
            * weights[chunk]
            * VOLUME
            * (grown * grown * grown - size * size * size),
        )

    def nucleate(sub):
        chunk = parcel_chunks + sub
        set_mass(chunk, evcount[sub] * NUCLEATE * softplus(local[chunk] - 1.0))

    def scatter(chunk):
        lines = hot_l[chunk]
        tops, rests = [], []
        for j in range(ROWS):
            block = lines[:, LANES * j : LANES * (j + 1)]
            top = jnp.broadcast_to(mass_hi[chunk, pl.ds(j, 1), :], (ny, LANES))
            rest = jnp.broadcast_to(mass_lo[chunk, pl.ds(j, 1), :], (ny, LANES))
            tops.append(block * top.astype(BF16))
            rests.append(block * rest.astype(BF16))
        left = jnp.concatenate(
            [jnp.concatenate(tops, axis=1), jnp.concatenate(rests, axis=1)], axis=0
        )
        return jnp.dot(left, hot_t[chunk], preferred_element_type=F32)

    def substep(sub, parcels, with_events, total):
        chunks = list(parcels)
        for chunk in chunks:
            gather(chunk)
        if with_events:
            gather(parcel_chunks + sub)
        for chunk in chunks:
            grow(chunk)
        if with_events:
            nucleate(sub)
            chunks.append(parcel_chunks + sub)
        return chunks

    def deposit(chunks, total):
        for chunk in chunks:
            total = total + scatter(chunk)
        return total

    def take(total):
        field[...] = field[...] - (total[:ny] + total[ny:])

    lane = lax.broadcasted_iota(I32, (ny, nz), 1)
    line = lax.broadcasted_iota(I32, (ny, nz), 0)

    def mix(step):
        plane = field[...]
        plane_out[step] = plane
        first = remote(5 + 2 * step, plane_out.at[step], halo.at[step, 0], partner)
        second = remote(6 + 2 * step, plane_out.at[step], halo.at[step, 1], other)
        return (first, second)

    def mixed(step, copies):
        plane = field[...]
        beside = jnp.where(line == 0, 0.0, pltpu.roll(plane, 1, 0))
        beside = beside + jnp.where(line == ny - 1, 0.0, pltpu.roll(plane, ny - 1, 0))
        beside = beside + jnp.where(lane == 0, 0.0, pltpu.roll(plane, 1, 1))
        beside = beside + jnp.where(lane == nz - 1, 0.0, pltpu.roll(plane, nz - 1, 1))
        for copy in copies:
            copy.wait_recv()
        at_end = jnp.logical_or(
            jnp.logical_and(s == 0, g == 0), jnp.logical_and(s == slabs - 1, g == 1)
        )
        inside = jnp.where(at_end, 0.0, 1.0)
        beside = beside + halo[step, 0] + halo[step, 1] * inside
        plane = plane + DIFFUSE * (beside - 6.0 * plane)
        return plane + inlet[...].astype(F32) * (INLET - plane)

    own = range(half)
    theirs = range(half, parcel_chunks)
    zero = jnp.zeros((2 * ny, nz), F32)

    build_parcels(0, half)
    for copy in loads[1:]:
        copy.wait()
    split_field()
    total = deposit(substep(0, own, False, None), zero)
    for copy in entry:
        copy.wait_recv()
    build_parcels(half, parcel_chunks)
    build_events(0)
    build_events(1)
    total = deposit(substep(0, theirs, True, None), total)
    take(total)
    split_field()
    every = range(parcel_chunks)
    take(deposit(substep(1, every, True, None), zero))
    planes = list(mix(0))
    build_events(2)
    build_events(3)
    slots = mrows.shape[1]
    down_lanes = lax.broadcasted_iota(I32, (LANES, slots), 0)
    down_rows = lax.broadcasted_iota(I32, (half * ROWS, slots), 0)
    slot = lax.broadcasted_iota(I32, (1, slots), 1)
    for j in range(2):
        rows = mrows[pl.ds(j, 1), :]
        mig_hot[j] = jnp.where(down_lanes == (rows & (LANES - 1)), 1.0, 0.0).astype(
            BF16
        )
        used = slot < mcount_ref[0, j]
        mig_line[j] = jnp.where(
            jnp.logical_and(down_rows == (rows >> 7), used), 1.0, 0.0
        )

    def pick(j, table):
        flat = jnp.concatenate(pieces(table, 3), axis=0)
        both = jnp.dot(flat, mig_hot[j], preferred_element_type=F32)
        count = half * ROWS
        read = both[:count] + both[count : 2 * count] + both[2 * count :]
        return jnp.sum(read * mig_line[j], axis=0, keepdims=True)

    weight_table = weights[pl.ds(0, half)].reshape(half * ROWS, LANES)
    for j in range(2):
        mig_out[j, pl.ds(1, 1), :] = pick(j, weight_table)
    field[...] = mixed(0, planes)
    split_field()
    take(deposit(substep(2, every, True, None), zero))
    split_field()
    chunks = substep(3, every, True, None)
    size_send[...] = sizes[pl.ds(half, half)]
    sent_back = remote(9, size_send, back, partner)
    take(deposit(chunks, zero))
    planes += list(mix(1))
    sent_back.wait_recv()
    own_line = (cells[pl.ds(0, half)] - base) >> shift
    here = jnp.logical_and(own_line >= 0, own_line < ny)
    final = jnp.where(here, sizes[pl.ds(0, half)], back[...])
    final = jnp.where(is_live, final, 0.0)
    size_ref[...] = final
    table = final.reshape(half * ROWS, LANES)
    for j in range(2):
        mig_out[j, pl.ds(0, 1), :] = pick(j, table)
    to_down = remote(10, mig_out.at[0], mig_in.at[1], down)
    to_up = remote(11, mig_out.at[1], mig_in.at[0], up)
    field_ref[0] = mixed(1, planes[2:])
    to_down.wait_recv()
    to_up.wait_recv()
    arrive_ref[0, 0] = mig_in[0] * jnp.where(s == 0, 0.0, 1.0)
    arrive_ref[0, 1] = mig_in[1] * jnp.where(s == slabs - 1, 0.0, 1.0)
    for copy in entry + planes + [sent_back, to_down, to_up]:
        copy.wait_send()


def local(
    saturation,
    inlet_mask,
    crystal_size,
    crystal_weight,
    crystal_cell,
    live_count,
    nucleus_cell,
    nucleus_count,
    migrant_rows,
    migrant_count,
):
    _, ny, nz = saturation.shape
    parcels = crystal_size.shape[0]
    half = parcels // CHUNK
    subs, events = nucleus_cell.shape[1:]
    slots = migrant_rows.shape[2]
    tiles = (half, ROWS, LANES)
    chunks = 2 * half + subs
    vmem = pltpu.VMEM
    field, size_out, arrivals = pl.pallas_call(
        kernel,
        out_shape=(
            jax.ShapeDtypeStruct((1, ny, nz), F32),
            jax.ShapeDtypeStruct(tiles, F32),
            jax.ShapeDtypeStruct((1, 2, 2, slots), F32),
        ),
        in_specs=[pl.BlockSpec(memory_space=pltpu.SMEM)] * 2
        + [pl.BlockSpec(memory_space=pl.ANY)] * 8,
        out_specs=(pl.BlockSpec(memory_space=vmem),) * 3,
        scratch_shapes=[
            vmem((ny, nz), F32),
            vmem((ny, nz), I32),
            vmem((2 * half, ROWS, LANES), F32),
            vmem((2 * half, ROWS, LANES), F32),
            vmem((2 * half, ROWS, LANES), I32),
            vmem(tiles, I32),
            vmem((2, subs, events), I32),
            vmem((2, subs, events), I32),
            vmem((2, slots), I32),
            vmem((subs, ROWS, LANES), I32),
            vmem((subs, ROWS, LANES), F32),
            vmem((STEPS, 2, ny, nz), F32),
            vmem(tiles, F32),
            vmem((2, 2, slots), F32),
            vmem((2, 2, slots), F32),
            vmem((STEPS, ny, nz), F32),
            vmem(tiles, F32),
            vmem((chunks, nz, CHUNK), BF16),
            vmem((chunks, CHUNK, nz), BF16),
            vmem((chunks, ny, CHUNK), BF16),
            vmem((2 * ny, nz), BF16),
            vmem((chunks, ROWS, LANES), F32),
            vmem((chunks, ROWS, LANES), F32),
            vmem((chunks, ROWS, LANES), F32),
            vmem((2, LANES, slots), BF16),
            vmem((2, half * ROWS, slots), F32),
            pltpu.SemaphoreType.DMA((8,)),
            pltpu.SemaphoreType.DMA((12,)),
            pltpu.SemaphoreType.DMA((12,)),
        ],
        compiler_params=pltpu.CompilerParams(
            collective_id=0,
            has_side_effects=True,
            vmem_limit_bytes=48 * 1024 * 1024,
        ),
        name="mixer",
    )(
        live_count,
        migrant_count,
        saturation,
        inlet_mask,
        crystal_size.reshape(tiles),
        crystal_weight.reshape(tiles),
        crystal_cell.reshape(tiles),
        nucleus_cell,
        nucleus_count,
        migrant_rows,
    )
    return (field, size_out.reshape(parcels), arrivals)


def solution(mesh):
    rows = P(("slab", "grp"))
    return jax.shard_map(
        local,
        mesh=mesh,
        in_specs=(rows,) * 10,
        out_specs=(rows,) * 3,
        check_vma=False,
    )
```

time: 175 us -> 45.4 us (0.26)
  the two profiles are of different devices: /device:TPU:24 before, /device:TPU:32 now
where the time goes in v1:
time: 45.4 us; the launch traced here: 44.9 us
  Pallas kernels  35.8 us (79%)
  local copies, waits for them, and re-layouts  7.71 us (17%)
  between operations  1.33 us (3%)
    pallas_call x1, Pallas kernels, local(): pl.pallas_call(kernel, out_shape=(jax.ShapeDtypeStruct((1, ny, nz), F32),...  35.8 us
    unnamed x21, local copies, waits for them, and re-layouts  7.71 us

profile of v1, /device:TPU:32, one launch (start us, length us, event | category | flops | bytes accessed | tf_op | source)
XLA Modules:
  0.0 44.9 jit_solution(12862092069530427945)
XLA Ops:
  0.6 0.0 copy-start.7
  1.3 0.0 copy-start.8
  1.3 0.0 copy-done.7
  1.3 0.6 %copy-done.8 = s32[1,2]{1,0:T(1,128)S(1)} copy-done((s32[1,2]{1,0:T(1,128)S(1)}, s32[1,2]{1,0:T(1,128)}, u32[]{:S(2)}) %copy-start.8) | copy-done | bytes 32
  2.0 0.0 copy-start
  2.0 0.8 %copy-done = f32[1,64,256]{2,1,0:T(8,128)S(1)} copy-done((f32[1,64,256]{2,1,0:T(8,128)S(1)}, f32[1,64,256]{2,1,0:T(8,128)}, u32[]{:S(2)}) %copy-start) | copy-done | bytes 65560
  2.8 0.0 copy-start.1
  2.8 0.8 %copy-done.1 = s32[1,64,256]{2,1,0:T(8,128)S(1)} copy-done((s32[1,64,256]{2,1,0:T(8,128)S(1)}, s32[1,64,256]{2,1,0:T(8,128)}, u32[]{:S(2)}) %copy-start.1) | copy-done | bytes 65560
  3.6 0.0 copy-start.2
  3.6 0.7 %copy-done.2 = f32[4096]{0:T(1024)S(1)} copy-done((f32[4096]{0:T(1024)S(1)}, f32[4096]{0:T(1024)}, u32[]{:S(2)}) %copy-start.2) | copy-done | bytes 16408
  4.4 0.0 copy-start.3
  4.4 0.7 %copy-done.3 = f32[4096]{0:T(1024)S(1)} copy-done((f32[4096]{0:T(1024)S(1)}, f32[4096]{0:T(1024)}, u32[]{:S(2)}) %copy-start.3) | copy-done | bytes 16408
  5.1 0.0 copy-start.4
  5.1 0.7 %copy-done.4 = s32[4096]{0:T(1024)S(1)} copy-done((s32[4096]{0:T(1024)S(1)}, s32[4096]{0:T(1024)}, u32[]{:S(2)}) %copy-start.4) | copy-done | bytes 16408
  5.8 0.0 copy-start.5
  5.8 0.7 %copy-done.5 = s32[1,4,512]{2,1,0:T(4,128)S(1)} copy-done((s32[1,4,512]{2,1,0:T(4,128)S(1)}, s32[1,4,512]{2,1,0:T(4,128)}, u32[]{:S(2)}) %copy-start.5) | copy-done | bytes 8216
  6.5 0.0 copy-start.6
  6.5 0.7 %copy-done.6 = s32[1,4,512]{2,1,0:T(4,128)S(1)} copy-done((s32[1,4,512]{2,1,0:T(4,128)S(1)}, s32[1,4,512]{2,1,0:T(4,128)}, u32[]{:S(2)}) %copy-start.6) | copy-done | bytes 8216
  7.2 35.8 %mixer.1 = (f32[1,64,256]{2,1,0:T(8,128)S(1)}, f32[4,8,128]{2,1,0:T(8,128)S(1)}, f32[1,2,2,512]{3,2,1,0:T(2,128)S(1)}) custom-call(s32[1]{0:T(128)S(6)} %copy.16.live_ref, s32[1,2]{1,0:T(1,128)S(1)} %copy-done.8, f32[1,64,256]{2,1,0:T(8,128)S(1)} %copy-done, s32[1,64,256]{2,1,0:T(8,128)S(1)} %copy-done.1, f32[4,8,128]{2,1,0:T(8,128)S(1)} %bitcast.4, ...), custom_call_target="tpu_custom_call" | custom-call | tf_op jit(solution)/shard_map/mixer/pallas_call | solution.py:380
  43.0 0.6 %copy.17 = f32[1,64,256]{2,1,0:T(8,128)} copy(f32[1,64,256]{2,1,0:T(8,128)S(1)} %get-tuple-element.12) | data formatting | bytes 131072
  43.6 0.6 %copy.18 = f32[4096]{0:T(1024)} copy(f32[4096]{0:T(1024)S(1)} %bitcast.7) | data formatting | bytes 32768
  44.3 0.6 %copy.19 = f32[1,2,2,512]{3,2,1,0:T(2,128)} copy(f32[1,2,2,512]{3,2,1,0:T(2,128)S(1)} %get-tuple-element.14) | data formatting | bytes 16384
Async XLA Ops:
  0.6 0.7 %copy-start.7 = (s32[1,2,512]{2,1,0:T(2,128)S(1)}, s32[1,2,512]{2,1,0:T(2,128)}, u32[]{:S(2)}) copy-start(s32[1,2,512]{2,1,0:T(2,128)} %mrows_hbm.1) | copy-start | bytes 12292
  1.3 0.7 %copy-start.8 = (s32[1,2]{1,0:T(1,128)S(1)}, s32[1,2]{1,0:T(1,128)}, u32[]{:S(2)}) copy-start(s32[1,2]{1,0:T(1,128)} %mcount_ref.1) | copy-start | bytes 28
  2.0 0.8 %copy-start = (f32[1,64,256]{2,1,0:T(8,128)S(1)}, f32[1,64,256]{2,1,0:T(8,128)}, u32[]{:S(2)}) copy-start(f32[1,64,256]{2,1,0:T(8,128)} %sat_hbm.1) | copy-start | bytes 196612
  2.8 0.8 %copy-start.1 = (s32[1,64,256]{2,1,0:T(8,128)S(1)}, s32[1,64,256]{2,1,0:T(8,128)}, u32[]{:S(2)}) copy-start(s32[1,64,256]{2,1,0:T(8,128)} %inlet_hbm.1) | copy-start | bytes 196612
  3.6 0.7 %copy-start.2 = (f32[4096]{0:T(1024)S(1)}, f32[4096]{0:T(1024)}, u32[]{:S(2)}) copy-start(f32[4096]{0:T(1024)} %param.12) | copy-start | bytes 49156
  4.4 0.7 %copy-start.3 = (f32[4096]{0:T(1024)S(1)}, f32[4096]{0:T(1024)}, u32[]{:S(2)}) copy-start(f32[4096]{0:T(1024)} %param.13) | copy-start | bytes 49156
  5.1 0.7 %copy-start.4 = (s32[4096]{0:T(1024)S(1)}, s32[4096]{0:T(1024)}, u32[]{:S(2)}) copy-start(s32[4096]{0:T(1024)} %param.14) | copy-start | bytes 49156
  5.8 0.7 %copy-start.5 = (s32[1,4,512]{2,1,0:T(4,128)S(1)}, s32[1,4,512]{2,1,0:T(4,128)}, u32[]{:S(2)}) copy-start(s32[1,4,512]{2,1,0:T(4,128)} %ncell_hbm.1) | copy-start | bytes 24580
  6.5 0.7 %copy-start.6 = (s32[1,4,512]{2,1,0:T(4,128)S(1)}, s32[1,4,512]{2,1,0:T(4,128)}, u32[]{:S(2)}) copy-start(s32[1,4,512]{2,1,0:T(4,128)} %ncount_hbm.1) | copy-start | bytes 24580

commit v2 on v1

--- a/solution.py
+++ b/solution.py
@@ -37,7 +37,7 @@
 
 def kernel(
     live_ref,
-    mcount_ref,
+    mcount_hbm,
     sat_hbm,
     inlet_hbm,
     size_hbm,
@@ -49,6 +49,7 @@
     field_ref,
     size_ref,
     arrive_ref,
+    mcount_ref,
     field,
     inlet,
     sizes,
@@ -62,8 +63,10 @@
     evcount,
     halo,
     back,
-    mig_out,
-    mig_in,
+    mig_size,
+    mig_weight,
+    got_size,
+    got_weight,
     plane_out,
     size_send,
     hot_p,
@@ -87,14 +90,31 @@
     s = lax.axis_index("slab")
     g = lax.axis_index("grp")
     slabs = lax.axis_size("slab")
-    up = (lax.rem(s + 1, slabs), g)
-    down = (lax.rem(s + slabs - 1, slabs), g)
+    has_down = s > 0
+    has_up = s < slabs - 1
     partner = (s, 1 - g)
-    other = (lax.rem(s + slabs + 2 * g - 1, slabs), 1 - g)
+    other = (s + 2 * g - 1, 1 - g)
+    has_other = jnp.logical_or(
+        jnp.logical_and(g == 0, has_down), jnp.logical_and(g == 1, has_up)
+    )
+    at_end = jnp.logical_not(has_other)
 
     barrier = pltpu.get_barrier_semaphore()
-    for peer in (partner, other, up, down):
+
+    def greet(peer):
         pl.semaphore_signal(barrier, inc=1, device_id=peer, device_id_type=MESH)
+
+    greet(partner)
+
+    @pl.when(has_down)
+    def _():
+        greet((s - 1, g))
+        greet((s - 1, 1 - g))
+
+    @pl.when(has_up)
+    def _():
+        greet((s + 1, g))
+        greet((s + 1, 1 - g))
 
     loads = []
     for index, (source, target) in enumerate(
@@ -106,14 +126,21 @@
             (ncell_hbm.at[0], ncell.at[0]),
             (ncount_hbm.at[0], ncount.at[0]),
             (inlet_hbm.at[0], inlet),
-            (mrows_hbm.at[0], mrows),
+            (mrows_hbm.at[0], mrows.at[0]),
+            (mcount_hbm.at[0], mcount_ref.at[0]),
         )
     ):
         copy = pltpu.make_async_copy(source, target, local_sem.at[index])
         copy.start()
         loads.append(copy)
 
-    def remote(index, source, target, peer):
+    def when(condition, action):
+        if condition is None:
+            action()
+        else:
+            pl.when(condition)(action)
+
+    def remote(index, source, target, peer, sends=None):
         copy = pltpu.make_async_remote_copy(
             src_ref=source,
             dst_ref=target,
@@ -122,7 +149,7 @@
             device_id=peer,
             device_id_type=MESH,
         )
-        copy.start()
+        when(sends, copy.start)
         return copy
 
     loads[0].wait()
@@ -135,15 +162,6 @@
     is_live = row_of < live
     cells_in[...] = jnp.where(is_live, cells_in[...], -1)
     cells[pl.ds(0, half)] = cells_in[...]
-
-    pl.semaphore_wait(barrier, 4)
-    entry = [
-        remote(0, cells_in, cells.at[pl.ds(half, half)], partner),
-        remote(1, size_hbm, sizes.at[pl.ds(half, half)], partner),
-        remote(2, weight_hbm, weights.at[pl.ds(half, half)], partner),
-        remote(3, ncell_hbm.at[0], ncell.at[1], partner),
-        remote(4, ncount_hbm.at[0], ncount.at[1], partner),
-    ]
 
     base = g * plane_cells
     down_nz = lax.broadcasted_iota(I32, (nz, LANES), 0)
@@ -260,11 +278,15 @@
     line = lax.broadcasted_iota(I32, (ny, nz), 0)
 
     def mix(step):
-        plane = field[...]
-        plane_out[step] = plane
-        first = remote(5 + 2 * step, plane_out.at[step], halo.at[step, 0], partner)
-        second = remote(6 + 2 * step, plane_out.at[step], halo.at[step, 1], other)
-        return (first, second)
+        plane_out[step] = field[...]
+        source = plane_out.at[step]
+        return (
+            (remote(5 + 2 * step, source, halo.at[step, 0], partner), None),
+            (
+                remote(6 + 2 * step, source, halo.at[step, 1], other, has_other),
+                has_other,
+            ),
+        )
 
     def mixed(step, copies):
         plane = field[...]
@@ -272,13 +294,9 @@
         beside = beside + jnp.where(line == ny - 1, 0.0, pltpu.roll(plane, ny - 1, 0))
         beside = beside + jnp.where(lane == 0, 0.0, pltpu.roll(plane, 1, 1))
         beside = beside + jnp.where(lane == nz - 1, 0.0, pltpu.roll(plane, nz - 1, 1))
-        for copy in copies:
-            copy.wait_recv()
-        at_end = jnp.logical_or(
-            jnp.logical_and(s == 0, g == 0), jnp.logical_and(s == slabs - 1, g == 1)
-        )
-        inside = jnp.where(at_end, 0.0, 1.0)
-        beside = beside + halo[step, 0] + halo[step, 1] * inside
+        for copy, condition in copies:
+            when(condition, copy.wait_recv)
+        beside = beside + halo[step, 0] + halo[step, 1]
         plane = plane + DIFFUSE * (beside - 6.0 * plane)
         return plane + inlet[...].astype(F32) * (INLET - plane)
 
@@ -286,7 +304,31 @@
     theirs = range(half, parcel_chunks)
     zero = jnp.zeros((2 * ny, nz), F32)
 
+    @pl.when(at_end)
+    def _():
+        for step in range(STEPS):
+            halo[step, 1] = jnp.zeros((ny, nz), F32)
+
+    def clear(index):
+        got_size[index] = jnp.zeros(got_size.shape[1:], F32)
+        got_weight[index] = jnp.zeros(got_weight.shape[1:], F32)
+
+    pl.when(jnp.logical_not(has_down))(lambda: clear(0))
+    pl.when(jnp.logical_not(has_up))(lambda: clear(1))
+
     build_parcels(0, half)
+    pl.semaphore_wait(
+        barrier, 1 + 2 * has_down.astype(I32) + 2 * has_up.astype(I32)
+    )
+    theirs = pl.ds(half, half)
+    entry = [
+        remote(0, cells_in, cells.at[theirs], partner),
+        remote(1, size_hbm, sizes.at[theirs], partner),
+        remote(2, weight_hbm, weights.at[theirs], partner),
+        remote(3, ncell_hbm.at[0], ncell.at[1], partner),
+        remote(4, ncount_hbm.at[0], ncount.at[1], partner),
+        remote(9, mrows_hbm.at[0], mrows.at[1], partner),
+    ]
     for copy in loads[1:]:
         copy.wait()
     split_field()
@@ -296,65 +338,107 @@
     build_parcels(half, parcel_chunks)
     build_events(0)
     build_events(1)
-    total = deposit(substep(0, theirs, True, None), total)
+    total = deposit(substep(0, range(half, parcel_chunks), True, None), total)
     take(total)
     split_field()
     every = range(parcel_chunks)
     take(deposit(substep(1, every, True, None), zero))
-    planes = list(mix(0))
+    planes = mix(0)
+    slots = mrows.shape[2]
+    rows_of = half * ROWS
+    down_lanes = lax.broadcasted_iota(I32, (LANES, slots), 0)
+    down_rows = lax.broadcasted_iota(I32, (rows_of, slots), 0)
+    slot = lax.broadcasted_iota(I32, (1, slots), 1)
+    for side in range(2):
+        for j in range(2):
+            rows = mrows[side, pl.ds(j, 1), :]
+            mig_hot[side, j] = jnp.where(
+                down_lanes == (rows & (LANES - 1)), 1.0, 0.0
+            ).astype(BF16)
+            mig_line[side, j] = jnp.where(down_rows == (rows >> 7), 1.0, 0.0)
+
+    def pick(side, j, flat):
+        both = jnp.dot(flat, mig_hot[side, j], preferred_element_type=F32)
+        read = both[:rows_of] + both[rows_of : 2 * rows_of] + both[2 * rows_of :]
+        return jnp.sum(read * mig_line[side, j], axis=0, keepdims=True)
+
+    def flat_pieces(table):
+        return jnp.concatenate(pieces(table.reshape(rows_of, LANES), 3), axis=0)
+
+    flat = flat_pieces(weights[pl.ds(0, half)])
+    for j in range(2):
+        used = jnp.where(slot < mcount_ref[0, j], 1.0, 0.0)
+        mig_weight[j, pl.ds(0, 1), :] = used
+        mig_weight[j, pl.ds(1, 1), :] = pick(0, j, flat) * used
+    last = [
+        (remote(10, mig_weight.at[0], got_weight.at[1], (s - 1, g), has_down), has_down, has_up),
+        (remote(11, mig_weight.at[1], got_weight.at[0], (s + 1, g), has_up), has_up, has_down),
+    ]
     build_events(2)
     build_events(3)
-    slots = mrows.shape[1]
-    down_lanes = lax.broadcasted_iota(I32, (LANES, slots), 0)
-    down_rows = lax.broadcasted_iota(I32, (half * ROWS, slots), 0)
-    slot = lax.broadcasted_iota(I32, (1, slots), 1)
-    for j in range(2):
-        rows = mrows[pl.ds(j, 1), :]
-        mig_hot[j] = jnp.where(down_lanes == (rows & (LANES - 1)), 1.0, 0.0).astype(
-            BF16
-        )
-        used = slot < mcount_ref[0, j]
-        mig_line[j] = jnp.where(
-            jnp.logical_and(down_rows == (rows >> 7), used), 1.0, 0.0
-        )
-
-    def pick(j, table):
-        flat = jnp.concatenate(pieces(table, 3), axis=0)
-        both = jnp.dot(flat, mig_hot[j], preferred_element_type=F32)
-        count = half * ROWS
-        read = both[:count] + both[count : 2 * count] + both[2 * count :]
-        return jnp.sum(read * mig_line[j], axis=0, keepdims=True)
-
-    weight_table = weights[pl.ds(0, half)].reshape(half * ROWS, LANES)
-    for j in range(2):
-        mig_out[j, pl.ds(1, 1), :] = pick(j, weight_table)
     field[...] = mixed(0, planes)
     split_field()
     take(deposit(substep(2, every, True, None), zero))
     split_field()
     chunks = substep(3, every, True, None)
-    size_send[...] = sizes[pl.ds(half, half)]
-    sent_back = remote(9, size_send, back, partner)
+    size_send[...] = sizes[theirs]
+    sent_back = remote(12, size_send, back, partner)
     take(deposit(chunks, zero))
-    planes += list(mix(1))
+    planes = planes + mix(1)
+    for side in range(2):
+        at = pl.ds(side * half, half)
+        mine = (cells[at] - base) >> shift
+        here = jnp.logical_and(mine >= 0, mine < ny)
+        flat = flat_pieces(jnp.where(here, sizes[at], 0.0))
+        to = g if side == 0 else 1 - g
+        for j in range(2):
+            mig_size[side, j] = pick(side, j, flat)
+        last.append(
+            (
+                remote(13 + 2 * side, mig_size.at[side, 0], got_size.at[1, side], (s - 1, to), has_down),
+                has_down,
+                has_up,
+            )
+        )
+        last.append(
+            (
+                remote(14 + 2 * side, mig_size.at[side, 1], got_size.at[0, side], (s + 1, to), has_up),
+                has_up,
+                has_down,
+            )
+        )
     sent_back.wait_recv()
     own_line = (cells[pl.ds(0, half)] - base) >> shift
     here = jnp.logical_and(own_line >= 0, own_line < ny)
     final = jnp.where(here, sizes[pl.ds(0, half)], back[...])
-    final = jnp.where(is_live, final, 0.0)
-    size_ref[...] = final
-    table = final.reshape(half * ROWS, LANES)
-    for j in range(2):
-        mig_out[j, pl.ds(0, 1), :] = pick(j, table)
-    to_down = remote(10, mig_out.at[0], mig_in.at[1], down)
-    to_up = remote(11, mig_out.at[1], mig_in.at[0], up)
+    size_ref[...] = jnp.where(is_live, final, 0.0)
     field_ref[0] = mixed(1, planes[2:])
-    to_down.wait_recv()
-    to_up.wait_recv()
-    arrive_ref[0, 0] = mig_in[0] * jnp.where(s == 0, 0.0, 1.0)
-    arrive_ref[0, 1] = mig_in[1] * jnp.where(s == slabs - 1, 0.0, 1.0)
-    for copy in entry + planes + [sent_back, to_down, to_up]:
+    for copy, _, receives in last:
+        when(receives, copy.wait_recv)
+    for side in range(2):
+        used = got_weight[side, pl.ds(0, 1), :]
+        size = got_size[side, 0] + got_size[side, 1]
+        arrive_ref[0, side, pl.ds(0, 1), :] = size * used
+        arrive_ref[0, side, pl.ds(1, 1), :] = got_weight[side, pl.ds(1, 1), :]
+    for copy in entry + [sent_back]:
         copy.wait_send()
+    for copy, sends in planes:
+        when(sends, copy.wait_send)
+    for copy, sends, _ in last:
+        when(sends, copy.wait_send)
+
+
+def store(field_ref, size_ref, arrive_ref, field_out, size_out, arrive_out, sem):
+    copies = [
+        pltpu.make_async_copy(source, target, sem.at[index])
+        for index, (source, target) in enumerate(
+            ((field_ref, field_out), (size_ref, size_out), (arrive_ref, arrive_out))
+        )
+    ]
+    for copy in copies:
+        copy.start()
+    for copy in copies:
+        copy.wait()
 
 
 def local(
@@ -377,17 +461,20 @@
     tiles = (half, ROWS, LANES)
     chunks = 2 * half + subs
     vmem = pltpu.VMEM
-    field, size_out, arrivals = pl.pallas_call(
+    in_vmem = pl.BlockSpec(memory_space=vmem)
+    in_hbm = pl.BlockSpec(memory_space=pltpu.HBM)
+    shapes = (
+        jax.ShapeDtypeStruct((1, ny, nz), F32),
+        jax.ShapeDtypeStruct(tiles, F32),
+        jax.ShapeDtypeStruct((1, 2, 2, slots), F32),
+    )
+    results = pl.pallas_call(
         kernel,
-        out_shape=(
-            jax.ShapeDtypeStruct((1, ny, nz), F32),
-            jax.ShapeDtypeStruct(tiles, F32),
-            jax.ShapeDtypeStruct((1, 2, 2, slots), F32),
-        ),
-        in_specs=[pl.BlockSpec(memory_space=pltpu.SMEM)] * 2
-        + [pl.BlockSpec(memory_space=pl.ANY)] * 8,
-        out_specs=(pl.BlockSpec(memory_space=vmem),) * 3,
+        out_shape=shapes,
+        in_specs=[pl.BlockSpec(memory_space=pltpu.SMEM)] + [in_hbm] * 9,
+        out_specs=(in_vmem,) * 3,
         scratch_shapes=[
+            pltpu.SMEM((1, 2), I32),
             vmem((ny, nz), F32),
             vmem((ny, nz), I32),
             vmem((2 * half, ROWS, LANES), F32),
@@ -396,12 +483,14 @@
             vmem(tiles, I32),
             vmem((2, subs, events), I32),
             vmem((2, subs, events), I32),
-            vmem((2, slots), I32),
+            vmem((2, 2, slots), I32),
             vmem((subs, ROWS, LANES), I32),
             vmem((subs, ROWS, LANES), F32),
             vmem((STEPS, 2, ny, nz), F32),
             vmem(tiles, F32),
+            vmem((2, 2, 1, slots), F32),
             vmem((2, 2, slots), F32),
+            vmem((2, 2, 1, slots), F32),
             vmem((2, 2, slots), F32),
             vmem((STEPS, ny, nz), F32),
             vmem(tiles, F32),
@@ -412,30 +501,43 @@
             vmem((chunks, ROWS, LANES), F32),
             vmem((chunks, ROWS, LANES), F32),
             vmem((chunks, ROWS, LANES), F32),
-            vmem((2, LANES, slots), BF16),
-            vmem((2, half * ROWS, slots), F32),
-            pltpu.SemaphoreType.DMA((8,)),
-            pltpu.SemaphoreType.DMA((12,)),
-            pltpu.SemaphoreType.DMA((12,)),
+            vmem((2, 2, LANES, slots), BF16),
+            vmem((2, 2, half * ROWS, slots), F32),
+            pltpu.SemaphoreType.DMA((9,)),
+            pltpu.SemaphoreType.DMA((17,)),
+            pltpu.SemaphoreType.DMA((17,)),
         ],
         compiler_params=pltpu.CompilerParams(
             collective_id=0,
             has_side_effects=True,
-            vmem_limit_bytes=48 * 1024 * 1024,
+            vmem_limit_bytes=32 * 1024 * 1024,
         ),
         name="mixer",
     )(
         live_count,
-        migrant_count,
-        saturation,
-        inlet_mask,
-        crystal_size.reshape(tiles),
-        crystal_weight.reshape(tiles),
-        crystal_cell.reshape(tiles),
-        nucleus_cell,
-        nucleus_count,
-        migrant_rows,
+        *(
+            pltpu.with_memory_space_constraint(operand, pltpu.HBM)
+            for operand in (
+                migrant_count,
+                saturation,
+                inlet_mask,
+                crystal_size.reshape(tiles),
+                crystal_weight.reshape(tiles),
+                crystal_cell.reshape(tiles),
+                nucleus_cell,
+                nucleus_count,
+                migrant_rows,
+            )
+        )
     )
+    field, size_out, arrivals = pl.pallas_call(
+        store,
+        out_shape=shapes,
+        in_specs=[pl.BlockSpec(memory_space=pl.ANY)] * 3,
+        out_specs=(in_hbm,) * 3,
+        scratch_shapes=[pltpu.SemaphoreType.DMA((3,))],
+        name="store",
+    )(*(pltpu.with_memory_space_constraint(result, vmem) for result in results))
     return (field, size_out.reshape(parcels), arrivals)
 
 

time: 45.4 us -> 35.1 us (0.77)
  the two profiles are of different devices: /device:TPU:32 before, /device:TPU:24 now
where the time goes in v2:
time: 35.1 us; the launch traced here: 34.9 us
  Pallas kernels  33.6 us (96%)
  between operations  1.29 us (4%)
    pallas_call x1, Pallas kernels, local(): pl.pallas_call(kernel, out_shape=shapes, in_specs=[pl.BlockSpec(memory_sp...  32.9 us

profile of v2, /device:TPU:24, one launch (start us, length us, event | category | flops | bytes accessed | tf_op | source)
XLA Modules:
  0.0 34.9 jit_solution(933451642865817707)
XLA Ops:
  1.3 32.9 %mixer.1 = (f32[1,64,256]{2,1,0:T(8,128)S(1)}, f32[4,8,128]{2,1,0:T(8,128)S(1)}, f32[1,2,2,512]{3,2,1,0:T(2,128)S(1)}) custom-call(s32[1]{0:T(128)S(6)} %copy.13.live_ref, s32[1,2]{1,0:T(1,128)} %mcount_hbm.1, f32[1,64,256]{2,1,0:T(8,128)} %sat_hbm.1, s32[1,64,256]{2,1,0:T(8,128)} %inlet_hbm.1, f32[4,8,128]{2,1,0:T(8,128)} %bitcast.4, f32[4,8,128]{2,1,0:T(8,128)} %bitcast.5, ...), custom_call_target="tpu_custom_call" | custom-call | tf_op jit(solution)/shard_map/mixer/pallas_call | solution.py:471
  34.2 0.7 %store.1 = (f32[1,64,256]{2,1,0:T(8,128)}, f32[4,8,128]{2,1,0:T(8,128)}, f32[1,2,2,512]{3,2,1,0:T(2,128)}) custom-call(f32[1,64,256]{2,1,0:T(8,128)S(1)} %get-tuple-element.9.field_ref, f32[4,8,128]{2,1,0:T(8,128)S(1)} %get-tuple-element.10.size_ref, f32[1,2,2,512]{3,2,1,0:T(2,128)S(1)} %get-tuple-element.11.arrive_ref), custom_call_target="tpu_custom_call" | custom-call | tf_op jit(solution)/shard_map/store/pallas_call | solution.py:533

commit v3 on v2

v3 whole, which is shorter than its diff:
```python
import jax
import jax.numpy as jnp
from jax import lax
from jax.experimental import pallas as pl
from jax.experimental.pallas import tpu as pltpu
from jax.sharding import PartitionSpec as P

STEPS = 2
SUBS = 2
GROWTH = 0.08
VOLUME = 1.0
NUCLEATE = 0.02
DIFFUSE = 0.12
INLET = 4.0

LANES = 128
ROWS = 8
CHUNK = ROWS * LANES
MESH = pl.DeviceIdType.MESH
F32 = jnp.float32
BF16 = jnp.bfloat16
I32 = jnp.int32


def softplus(x):
    return jnp.maximum(x, 0.0) + jnp.log1p(jnp.exp(-jnp.abs(x)))


def pieces(x, count):
    out = []
    for _ in range(count):
        top = x.astype(BF16)
        out.append(top)
        x = x - top.astype(F32)
    return out


def when(condition, action):
    if condition is None:
        action()
    else:
        pl.when(condition)(action)


def greet(peer):
    barrier = pltpu.get_barrier_semaphore()
    pl.semaphore_signal(barrier, inc=1, device_id=peer, device_id_type=MESH)


class Hot:
    def __init__(self, base, ny, nz):
        self.base, self.ny, self.nz = base, ny, nz
        self.shift = nz.bit_length() - 1
        self.chunks = {}

    def add(self, first, refs):
        for index in range(refs[0].shape[0]):
            self.chunks[first + index] = (*refs, index)

    def build(self, chunk, tile):
        hot_p, hot_t, hot_l, at = self.chunks[chunk]
        cell = tile - self.base
        place = cell & (self.nz - 1)
        line = cell >> self.shift
        turned = jnp.transpose(place)
        down_nz = lax.broadcasted_iota(I32, (self.nz, LANES), 0)
        down_ny = lax.broadcasted_iota(I32, (self.ny, LANES), 0)
        along_nz = lax.broadcasted_iota(I32, (LANES, self.nz), 1)
        for j in range(ROWS):
            columns = pl.ds(LANES * j, LANES)
            hot_p[at, :, columns] = jnp.where(
                down_nz == place[j : j + 1, :], 1.0, 0.0
            ).astype(BF16)
            hot_l[at, :, columns] = jnp.where(
                down_ny == line[j : j + 1, :], 1.0, 0.0
            ).astype(BF16)
            hot_t[at, columns, :] = jnp.where(
                along_nz == jnp.broadcast_to(turned[:, j : j + 1], (LANES, self.nz)),
                1.0,
                0.0,
            ).astype(BF16)

    def here(self, cells):
        line = (cells - self.base) >> self.shift
        return jnp.logical_and(line >= 0, line < self.ny)

    def gather(self, chunk, pair, local):
        hot_p, _, hot_l, at = self.chunks[chunk]
        ny = self.ny
        both = jnp.dot(pair[...], hot_p[at], preferred_element_type=F32)
        read = (both[:ny] + both[ny:]) * hot_l[at].astype(F32)
        flat = jnp.sum(read, axis=0, keepdims=True)
        for j in range(ROWS):
            local[chunk, pl.ds(j, 1), :] = flat[:, LANES * j : LANES * (j + 1)]

    def scatter(self, chunk, mass):
        _, hot_t, hot_l, at = self.chunks[chunk]
        lines = hot_l[at]
        tops, rests = [], []
        for j in range(ROWS):
            block = lines[:, LANES * j : LANES * (j + 1)]
            row = (self.ny, LANES)
            top = jnp.broadcast_to(mass[chunk, 0, pl.ds(j, 1), :], row)
            rest = jnp.broadcast_to(mass[chunk, 1, pl.ds(j, 1), :], row)
            tops.append(block * top.astype(BF16))
            rests.append(block * rest.astype(BF16))
        left = jnp.concatenate(
            [jnp.concatenate(tops, axis=1), jnp.concatenate(rests, axis=1)], axis=0
        )
        return jnp.dot(left, hot_t[at], preferred_element_type=F32)


def set_mass(mass, chunk, value):
    top = value.astype(BF16).astype(F32)
    mass[chunk, 0] = top
    mass[chunk, 1] = value - top


def deposit(chunks, total, hot, pair, local, mass, weigh):
    for k in range(len(chunks) + 1):
        if k < len(chunks):
            hot.gather(chunks[k], pair, local)
            weigh(chunks[k])
        if k >= 1:
            total = total + hot.scatter(chunks[k - 1], mass)
    return total


def split(plane, pair):
    ny = plane.shape[0]
    top, rest = pieces(plane, 2)
    pair[pl.ds(0, ny), :] = top
    pair[pl.ds(ny, ny), :] = rest


def grower(hot, cells, sizes, weights, local, mass):
    def grow(chunk):
        here = jnp.where(hot.here(cells[chunk]), 1.0, 0.0)
        size = sizes[chunk]
        grown = size + here * GROWTH * softplus(local[chunk] - 1.0)
        sizes[chunk] = grown
        cubes = grown * grown * grown - size * size * size
        set_mass(mass, chunk, here * weights[chunk] * VOLUME * cubes)

    return grow


def event_tiles(sub, ncell, ncount):
    rows = ROWS // 2
    cell, count = [], []
    for side in range(2):
        for j in range(rows):
            columns = slice(LANES * j, LANES * (j + 1))
            cell.append(ncell[side, sub : sub + 1, columns])
            count.append(ncount[side, sub : sub + 1, columns])
    return jnp.concatenate(cell, axis=0), jnp.concatenate(count, axis=0).astype(F32)


def meet(
    live_ref,
    sat_hbm,
    size_hbm,
    weight_hbm,
    cell_hbm,
    ncell_hbm,
    ncount_hbm,
    mrows_hbm,
    field,
    sizes,
    weights,
    cells,
    ncell,
    ncount,
    mrows,
    total,
    hot_p,
    hot_t,
    hot_l,
    cells_in,
    got_cells,
    got_sizes,
    got_weights,
    got_ncell,
    got_ncount,
    got_mrows,
    pair,
    local,
    mass,
    local_sem,
    send_sem,
    recv_sem,
):
    ny, nz = field.shape
    half = cells_in.shape[0]
    s = lax.axis_index("slab")
    g = lax.axis_index("grp")
    partner = (s, 1 - g)
    greet(partner)
    mine = pl.ds(0, half)
    loads = []
    for index, (source, target) in enumerate(
        (
            (cell_hbm, cells_in),
            (sat_hbm.at[0], field),
            (size_hbm, sizes.at[mine]),
            (weight_hbm, weights.at[mine]),
            (ncell_hbm.at[0], ncell.at[0]),
            (ncount_hbm.at[0], ncount.at[0]),
            (mrows_hbm.at[0], mrows.at[0]),
        )
    ):
        copy = pltpu.make_async_copy(source, target, local_sem.at[index])
        copy.start()
        loads.append(copy)

    loads[0].wait()
    live = live_ref[0]
    tiles = cells_in.shape
    row_of = (
        lax.broadcasted_iota(I32, tiles, 0) * CHUNK
        + lax.broadcasted_iota(I32, tiles, 1) * LANES
        + lax.broadcasted_iota(I32, tiles, 2)
    )
    own_cells = jnp.where(row_of < live, cells_in[...], -1)
    cells_in[...] = own_cells
    cells[mine] = own_cells

    pl.semaphore_wait(pltpu.get_barrier_semaphore(), 1)
    entry = []
    for index, (source, target) in enumerate(
        (
            (cells_in, got_cells),
            (ncell_hbm.at[0], got_ncell),
            (size_hbm, got_sizes),
            (weight_hbm, got_weights),
            (ncount_hbm.at[0], got_ncount),
            (mrows_hbm.at[0], got_mrows),
        )
    ):
        copy = pltpu.make_async_remote_copy(
            src_ref=source,
            dst_ref=target,
            send_sem=send_sem.at[index],
            recv_sem=recv_sem.at[index],
            device_id=partner,
            device_id_type=MESH,
        )
        copy.start()
        entry.append(copy)

    hot = Hot(g * (ny * nz), ny, nz)
    hot.add(0, (hot_p, hot_t, hot_l))
    for chunk in range(half):
        hot.build(chunk, cells[chunk])
    for copy in loads[1:]:
        copy.wait()
    split(field[...], pair)
    grow = grower(hot, cells, sizes, weights, local, mass)
    zero = jnp.zeros((2 * ny, nz), F32)
    total[...] = deposit(list(range(half)), zero, hot, pair, local, mass, grow)

    theirs = pl.ds(half, half)
    entry[0].wait_recv()
    cells[theirs] = got_cells[...]
    for chunk in range(half, 2 * half):
        hot.build(chunk, cells[chunk])
    entry[1].wait_recv()
    ncell[1] = got_ncell[...]
    for copy in entry[2:]:
        copy.wait_recv()
    sizes[theirs] = got_sizes[...]
    weights[theirs] = got_weights[...]
    ncount[1] = got_ncount[...]
    mrows[1] = got_mrows[...]
    for sub in range(SUBS):
        hot.build(2 * half + sub, event_tiles(sub, ncell, ncount)[0])
    for copy in entry:
        copy.wait_send()


def run(
    mcount_hbm,
    inlet_hbm,
    field_in,
    sizes_in,
    weights,
    cells,
    ncell,
    ncount,
    mrows,
    total_in,
    hot_p,
    hot_t,
    hot_l,
    field_ref,
    size_ref,
    arrive_ref,
    mcount_ref,
    inlet,
    field,
    sizes,
    halo,
    back,
    mig_size,
    mig_weight,
    got_size,
    got_weight,
    plane_out,
    size_send,
    late_p,
    late_t,
    late_l,
    pair,
    local,
    mass,
    evcount,
    mig_hot,
    mig_line,
    local_sem,
    send_sem,
    recv_sem,
):
    ny, nz = field.shape
    half = back.shape[0]
    parcel_chunks = 2 * half
    s = lax.axis_index("slab")
    g = lax.axis_index("grp")
    slabs = lax.axis_size("slab")
    has_down = s > 0
    has_up = s < slabs - 1
    partner = (s, 1 - g)
    other = (s + 2 * g - 1, 1 - g)
    has_other = jnp.logical_or(
        jnp.logical_and(g == 0, has_down), jnp.logical_and(g == 1, has_up)
    )

    def greet_slab(slab):
        greet((slab, g))
        greet((slab, 1 - g))

    pl.when(has_down)(lambda: greet_slab(s - 1))
    pl.when(has_up)(lambda: greet_slab(s + 1))
    greet(partner)
    loads = []
    for index, (source, target) in enumerate(
        ((mcount_hbm.at[0], mcount_ref.at[0]), (inlet_hbm.at[0], inlet))
    ):
        copy = pltpu.make_async_copy(source, target, local_sem.at[index])
        copy.start()
        loads.append(copy)

    def remote(index, source, target, peer, sends=None):
        copy = pltpu.make_async_remote_copy(
            src_ref=source,
            dst_ref=target,
            send_sem=send_sem.at[index],
            recv_sem=recv_sem.at[index],
            device_id=peer,
            device_id_type=MESH,
        )
        when(sends, copy.start)
        return copy

    hot = Hot(g * (ny * nz), ny, nz)
    hot.add(0, (hot_p, hot_t, hot_l))
    hot.add(hot_p.shape[0], (late_p, late_t, late_l))
    sizes[...] = sizes_in[...]
    grow = grower(hot, cells, sizes, weights, local, mass)

    def weigh(chunk):
        if chunk < parcel_chunks:
            grow(chunk)
        else:
            made = evcount[chunk - parcel_chunks]
            set_mass(mass, chunk, made * NUCLEATE * softplus(local[chunk] - 1.0))

    for sub in range(STEPS * SUBS):
        evcount[sub] = event_tiles(sub, ncell, ncount)[1]

    def substep(plane, chunks, total):
        split(plane, pair)
        total = deposit(chunks, total, hot, pair, local, mass, weigh)
        field[...] = plane - (total[:ny] + total[ny:])

    lane = lax.broadcasted_iota(I32, (ny, nz), 1)
    line = lax.broadcasted_iota(I32, (ny, nz), 0)

    def mix(step):
        plane_out[step] = field[...]
        source = plane_out.at[step]
        first = remote(2 * step, source, halo.at[step, 0], partner)
        second = remote(2 * step + 1, source, halo.at[step, 1], other, has_other)
        return ((first, None), (second, has_other))

    def mixed(step, copies):
        plane = field[...]
        beside = jnp.where(line == 0, 0.0, pltpu.roll(plane, 1, 0))
        beside = beside + jnp.where(line == ny - 1, 0.0, pltpu.roll(plane, ny - 1, 0))
        beside = beside + jnp.where(lane == 0, 0.0, pltpu.roll(plane, 1, 1))
        beside = beside + jnp.where(lane == nz - 1, 0.0, pltpu.roll(plane, nz - 1, 1))
        for copy, condition in copies:
            when(condition, copy.wait_recv)
        beside = beside + halo[step, 0] + halo[step, 1]
        plane = plane + DIFFUSE * (beside - 6.0 * plane)
        return plane + inlet[...].astype(F32) * (INLET - plane)

    @pl.when(jnp.logical_not(has_other))
    def _():
        for step in range(STEPS):
            halo[step, 1] = jnp.zeros((ny, nz), F32)

    def clear(index):
        got_size[index] = jnp.zeros(got_size.shape[1:], F32)
        got_weight[index] = jnp.zeros(got_weight.shape[1:], F32)

    pl.when(jnp.logical_not(has_down))(lambda: clear(0))
    pl.when(jnp.logical_not(has_up))(lambda: clear(1))

    every = list(range(parcel_chunks))
    zero = jnp.zeros((2 * ny, nz), F32)
    substep(field_in[...], every[half:] + [parcel_chunks], total_in[...])
    substep(field[...], every + [parcel_chunks + 1], zero)
    for copy in loads:
        copy.wait()
    pl.semaphore_wait(
        pltpu.get_barrier_semaphore(),
        1 + 2 * has_down.astype(I32) + 2 * has_up.astype(I32),
    )
    planes = mix(0)
    slots = mrows.shape[2]
    rows_of = half * ROWS
    down_lanes = lax.broadcasted_iota(I32, (LANES, slots), 0)
    down_rows = lax.broadcasted_iota(I32, (rows_of, slots), 0)
    slot = lax.broadcasted_iota(I32, (1, slots), 1)
    for side in range(2):
        for j in range(2):
            rows = mrows[side, pl.ds(j, 1), :]
            mig_hot[side, j] = jnp.where(
                down_lanes == (rows & (LANES - 1)), 1.0, 0.0
            ).astype(BF16)
            mig_line[side, j] = jnp.where(down_rows == (rows >> 7), 1.0, 0.0)

    def pick(side, j, flat):
        both = jnp.dot(flat, mig_hot[side, j], preferred_element_type=F32)
        read = both[:rows_of] + both[rows_of : 2 * rows_of] + both[2 * rows_of :]
        return jnp.sum(read * mig_line[side, j], axis=0, keepdims=True)

    def flat_pieces(table):
        return jnp.concatenate(pieces(table.reshape(rows_of, LANES), 3), axis=0)

    flat = flat_pieces(weights[pl.ds(0, half)])
    for j in range(2):
        used = jnp.where(slot < mcount_ref[0, j], 1.0, 0.0)
        mig_weight[j, pl.ds(0, 1), :] = used
        mig_weight[j, pl.ds(1, 1), :] = pick(0, j, flat) * used
    last = []

    def send_both(index, source, target, grp):
        low = remote(index, source[0], target[1], (s - 1, grp), has_down)
        high = remote(index + 1, source[1], target[0], (s + 1, grp), has_up)
        last.append((low, has_down, has_up))
        last.append((high, has_up, has_down))

    send_both(
        4,
        (mig_weight.at[0], mig_weight.at[1]),
        (got_weight.at[0], got_weight.at[1]),
        g,
    )
    for sub in range(SUBS, STEPS * SUBS):
        hot.build(parcel_chunks + sub, event_tiles(sub, ncell, ncount)[0])
    substep(mixed(0, planes), every + [parcel_chunks + 2], zero)
    substep(field[...], every + [parcel_chunks + 3], zero)
    planes = planes + mix(1)
    theirs = pl.ds(half, half)
    size_send[...] = sizes[theirs]
    sent_back = remote(6, size_send, back, partner)
    for side in range(2):
        at = pl.ds(side * half, half)
        flat = flat_pieces(jnp.where(hot.here(cells[at]), sizes[at], 0.0))
        for j in range(2):
            mig_size[side, j] = pick(side, j, flat)
        send_both(
            7 + 2 * side,
            (mig_size.at[side, 0], mig_size.at[side, 1]),
            (got_size.at[0, side], got_size.at[1, side]),
            g if side == 0 else 1 - g,
        )
    sent_back.wait_recv()
    mine = pl.ds(0, half)
    final = jnp.where(hot.here(cells[mine]), sizes[mine], back[...])
    size_ref[...] = jnp.where(cells[mine] >= 0, final, 0.0)
    field_ref[0] = mixed(1, planes[2:])
    for copy, _, receives in last:
        when(receives, copy.wait_recv)
    for side in range(2):
        used = got_weight[side, pl.ds(0, 1), :]
        size = got_size[side, 0] + got_size[side, 1]
        arrive_ref[0, side, pl.ds(0, 1), :] = size * used
        arrive_ref[0, side, pl.ds(1, 1), :] = got_weight[side, pl.ds(1, 1), :]
    sent_back.wait_send()
    for copy, sends in planes:
        when(sends, copy.wait_send)
    for copy, sends, _ in last:
        when(sends, copy.wait_send)


def store(field_ref, size_ref, arrive_ref, field_out, size_out, arrive_out, sem):
    copies = [
        pltpu.make_async_copy(source, target, sem.at[index])
        for index, (source, target) in enumerate(
            ((field_ref, field_out), (size_ref, size_out), (arrive_ref, arrive_out))
        )
    ]
    for copy in copies:
        copy.start()
    for copy in copies:
        copy.wait()


def local(
    saturation,
    inlet_mask,
    crystal_size,
    crystal_weight,
    crystal_cell,
    live_count,
    nucleus_cell,
    nucleus_count,
    migrant_rows,
    migrant_count,
):
    _, ny, nz = saturation.shape
    parcels = crystal_size.shape[0]
    half = parcels // CHUNK
    subs, events = nucleus_cell.shape[1:]
    slots = migrant_rows.shape[2]
    tiles = (half, ROWS, LANES)
    both = (2 * half, ROWS, LANES)
    chunks = 2 * half + subs
    early = 2 * half + SUBS
    vmem = pltpu.VMEM
    dma = pltpu.SemaphoreType.DMA
    in_smem = pl.BlockSpec(memory_space=pltpu.SMEM)
    in_vmem = pl.BlockSpec(memory_space=vmem)
    in_hbm = pl.BlockSpec(memory_space=pltpu.HBM)
    anywhere = pl.BlockSpec(memory_space=pl.ANY)

    def kept(*arrays):
        return [pltpu.with_memory_space_constraint(a, pltpu.HBM) for a in arrays]

    def close(arrays):
        return [pltpu.with_memory_space_constraint(a, vmem) for a in arrays]

    def params(index):
        return pltpu.CompilerParams(
            collective_id=index,
            has_side_effects=True,
            vmem_limit_bytes=20 * 1024 * 1024,
        )

    shape = jax.ShapeDtypeStruct
    met = pl.pallas_call(
        meet,
        out_shape=(
            shape((ny, nz), F32),
            shape(both, F32),
            shape(both, F32),
            shape(both, I32),
            shape((2, subs, events), I32),
            shape((2, subs, events), I32),
            shape((2, 2, slots), I32),
            shape((2 * ny, nz), F32),
            shape((early, nz, CHUNK), BF16),
            shape((early, CHUNK, nz), BF16),
            shape((early, ny, CHUNK), BF16),
        ),
        in_specs=[in_smem] + [in_hbm] * 7,
        out_specs=(in_vmem,) * 11,
        scratch_shapes=[
            vmem(tiles, I32),
            vmem(tiles, I32),
            vmem(tiles, F32),
            vmem(tiles, F32),
            vmem((subs, events), I32),
            vmem((subs, events), I32),
            vmem((2, slots), I32),
            vmem((2 * ny, nz), BF16),
            vmem((chunks, ROWS, LANES), F32),
            vmem((chunks, 2, ROWS, LANES), F32),
            dma((7,)),
            dma((6,)),
            dma((6,)),
        ],
        compiler_params=params(0),
        name="meet",
    )(
        live_count,
        *kept(
            saturation,
            crystal_size.reshape(tiles),
            crystal_weight.reshape(tiles),
            crystal_cell.reshape(tiles),
            nucleus_cell,
            nucleus_count,
            migrant_rows,
        ),
    )
    shapes = (
        shape((1, ny, nz), F32),
        shape(tiles, F32),
        shape((1, 2, 2, slots), F32),
    )
    results = pl.pallas_call(
        run,
        out_shape=shapes,
        in_specs=[in_hbm] * 2 + [in_vmem] * 11,
        out_specs=(in_vmem,) * 3,
        scratch_shapes=[
            pltpu.SMEM((1, 2), I32),
            vmem((ny, nz), I32),
            vmem((ny, nz), F32),
            vmem(both, F32),
            vmem((STEPS, 2, ny, nz), F32),
            vmem(tiles, F32),
            vmem((2, 2, 1, slots), F32),
            vmem((2, 2, slots), F32),
            vmem((2, 2, 1, slots), F32),
            vmem((2, 2, slots), F32),
            vmem((STEPS, ny, nz), F32),
            vmem(tiles, F32),
            vmem((chunks - early, nz, CHUNK), BF16),
            vmem((chunks - early, CHUNK, nz), BF16),
            vmem((chunks - early, ny, CHUNK), BF16),
            vmem((2 * ny, nz), BF16),
            vmem((chunks, ROWS, LANES), F32),
            vmem((chunks, 2, ROWS, LANES), F32),
            vmem((subs, ROWS, LANES), F32),
            vmem((2, 2, LANES, slots), BF16),
            vmem((2, 2, half * ROWS, slots), F32),
            dma((2,)),
            dma((11,)),
            dma((11,)),
        ],
        compiler_params=params(1),
        name="run",
    )(*kept(migrant_count, inlet_mask), *close(met))
    field, size_out, arrivals = pl.pallas_call(
        store,
        out_shape=shapes,
        in_specs=[anywhere] * 3,
        out_specs=(in_hbm,) * 3,
        scratch_shapes=[dma((3,))],
        name="store",
    )(*close(results))
    return (field, size_out.reshape(parcels), arrivals)


def solution(mesh):
    rows = P(("slab", "grp"))
    return jax.shard_map(
        local,
        mesh=mesh,
        in_specs=(rows,) * 10,
        out_specs=(rows,) * 3,
        check_vma=False,
    )
```

time: 35.1 us -> 32.6 us (0.929)
  Pallas kernels: 33.6 us -> 30.9 us
    pallas_call x2 -> x3, Pallas kernels: 33.6 us -> 30.9 us  [the longest x1 22.5 us: local(): pl.pallas_call(run, out_shape=shapes, in_specs=[in_hbm] * 2 + [in_vmem] *...]
where the time goes in v3:
time: 32.6 us; the launch traced here: 32.4 us
  Pallas kernels  30.9 us (95%)
  between operations  1.45 us (4%)
    pallas_call x1, Pallas kernels, local(): pl.pallas_call(run, out_shape=shapes, in_specs=[in_hbm] * 2 + [in_vmem] *...  22.5 us
    pallas_call x1, Pallas kernels, local(): pl.pallas_call(meet, out_shape=(shape((ny, nz), F32), shape(both, F32), s...  7.75 us
    pallas_call x1, Pallas kernels, local(): pl.pallas_call(store, out_shape=shapes, in_specs=[anywhere] * 3, out_spec...  0.66 us

profile of v3, /device:TPU:24, one launch (start us, length us, event | category | flops | bytes accessed | tf_op | source)
XLA Modules:
  0.0 32.4 jit_solution(10702610291603958200)
XLA Ops:
  1.3 7.8 %meet.1 = (f32[64,256]{1,0:T(8,128)S(1)}, f32[8,8,128]{2,1,0:T(8,128)S(1)}, f32[8,8,128]{2,1,0:T(8,128)S(1)}, s32[8,8,128]{2,1,0:T(8,128)S(1)}, s32[2,4,512]{2,1...) custom-call(s32[1]{0:T(128)S(6)} %copy.13.live_ref, ...), custom_call_target="tpu_custom_call" | custom-call | tf_op jit(solution)/shard_map/meet/pallas_call | solution.py:563
  9.0 22.5 %run.1 = (f32[1,64,256]{2,1,0:T(8,128)S(1)}, f32[4,8,128]{2,1,0:T(8,128)S(1)}, f32[1,2,2,512]{3,2,1,0:T(2,128)S(1)}) custom-call(s32[1,2]{1,0:T(1,128)} %mcount_hbm.1, s32[1,64,256]{2,1,0:T(8,128)} %inlet_hbm.1, f32[64,256]{1,0:T(8,128)S(1)} %get-tuple-element.20.field_in, f32[8,8,128]{2,1,0:T(8,128)S(1)} %get-tuple-element.21.sizes_in, ...), custom_call_target="tpu_custom_call" | custom-call | tf_op jit(solution)/shard_map/run/pallas_call | solution.py:614
  31.6 0.7 %store.1 = (f32[1,64,256]{2,1,0:T(8,128)}, f32[4,8,128]{2,1,0:T(8,128)}, f32[1,2,2,512]{3,2,1,0:T(2,128)}) custom-call(f32[1,64,256]{2,1,0:T(8,128)S(1)} %get-tuple-element.31.field_ref, f32[4,8,128]{2,1,0:T(8,128)S(1)} %get-tuple-element.32.size_ref, f32[1,2,2,512]{3,2,1,0:T(2,128)S(1)} %get-tuple-element.33.arrive_ref), custom_call_target="tpu_custom_call" | custom-call | tf_op jit(solution)/shard_map/store/pallas_call | solution.py:648

commit v4 on v3

--- a/solution.py
+++ b/solution.py
@@ -16,6 +16,8 @@
 LANES = 128
 ROWS = 8
 CHUNK = ROWS * LANES
+EARLY = 1
+LAG = 1
 MESH = pl.DeviceIdType.MESH
 F32 = jnp.float32
 BF16 = jnp.bfloat16
@@ -62,23 +64,32 @@
         cell = tile - self.base
         place = cell & (self.nz - 1)
         line = cell >> self.shift
-        turned = jnp.transpose(place)
-        down_nz = lax.broadcasted_iota(I32, (self.nz, LANES), 0)
-        down_ny = lax.broadcasted_iota(I32, (self.ny, LANES), 0)
-        along_nz = lax.broadcasted_iota(I32, (LANES, self.nz), 1)
+        placed, lined = place.astype(F32), line.astype(F32)
+        turned = jnp.transpose(placed)
+
+        def iota(shape, dim):
+            return lax.broadcasted_iota(I32, shape, dim).astype(F32).astype(BF16)
+
+        down_nz = iota((self.nz, LANES), 0)
+        down_ny = iota((self.ny, LANES), 0)
+        along_nz = iota((LANES, self.nz), 1)
+        one, none = jnp.ones((), BF16), jnp.zeros((), BF16)
         for j in range(ROWS):
             columns = pl.ds(LANES * j, LANES)
+
+            def spread(row, shape):
+                return jnp.broadcast_to(row, shape).astype(BF16)
+
+            row = slice(j, j + 1)
             hot_p[at, :, columns] = jnp.where(
-                down_nz == place[j : j + 1, :], 1.0, 0.0
-            ).astype(BF16)
+                down_nz == spread(placed[row, :], down_nz.shape), one, none
+            )
             hot_l[at, :, columns] = jnp.where(
-                down_ny == line[j : j + 1, :], 1.0, 0.0
-            ).astype(BF16)
+                down_ny == spread(lined[row, :], down_ny.shape), one, none
+            )
             hot_t[at, columns, :] = jnp.where(
-                along_nz == jnp.broadcast_to(turned[:, j : j + 1], (LANES, self.nz)),
-                1.0,
-                0.0,
-            ).astype(BF16)
+                along_nz == spread(turned[:, row], along_nz.shape), one, none
+            )
 
     def here(self, cells):
         line = (cells - self.base) >> self.shift
@@ -442,13 +453,15 @@
 
     def pick(side, j, flat):
         both = jnp.dot(flat, mig_hot[side, j], preferred_element_type=F32)
-        read = both[:rows_of] + both[rows_of : 2 * rows_of] + both[2 * rows_of :]
+        read = sum(
+            both[at : at + rows_of] for at in range(0, flat.shape[0], rows_of)
+        )
         return jnp.sum(read * mig_line[side, j], axis=0, keepdims=True)
 
-    def flat_pieces(table):
-        return jnp.concatenate(pieces(table.reshape(rows_of, LANES), 3), axis=0)
-
-    flat = flat_pieces(weights[pl.ds(0, half)])
+    def flat_pieces(table, count):
+        return jnp.concatenate(pieces(table.reshape(rows_of, LANES), count), axis=0)
+
+    flat = flat_pieces(weights[pl.ds(0, half)], 3)
     for j in range(2):
         used = jnp.where(slot < mcount_ref[0, j], 1.0, 0.0)
         mig_weight[j, pl.ds(0, 1), :] = used
@@ -470,22 +483,39 @@
     for sub in range(SUBS, STEPS * SUBS):
         hot.build(parcel_chunks + sub, event_tiles(sub, ncell, ncount)[0])
     substep(mixed(0, planes), every + [parcel_chunks + 2], zero)
-    substep(field[...], every + [parcel_chunks + 3], zero)
-    planes = planes + mix(1)
-    theirs = pl.ds(half, half)
-    size_send[...] = sizes[theirs]
-    sent_back = remote(6, size_send, back, partner)
+    plane = field[...]
+    split(plane, pair)
+    events = parcel_chunks + 3
+    total = zero
+    done = 0
+    for chunk in [events] + every:
+        hot.gather(chunk, pair, local)
+        weigh(chunk)
+        if chunk < events and chunk >= LAG:
+            total = total + hot.scatter(chunk - LAG, mass)
+            done = chunk - LAG + 1
     for side in range(2):
         at = pl.ds(side * half, half)
-        flat = flat_pieces(jnp.where(hot.here(cells[at]), sizes[at], 0.0))
+        flat = flat_pieces(jnp.where(hot.here(cells[at]), sizes[at], 0.0), 2)
         for j in range(2):
             mig_size[side, j] = pick(side, j, flat)
+    rest = every[done:] + [events]
+    for chunk in rest[:EARLY]:
+        total = total + hot.scatter(chunk, mass)
+    for side in range(2):
         send_both(
             7 + 2 * side,
             (mig_size.at[side, 0], mig_size.at[side, 1]),
             (got_size.at[0, side], got_size.at[1, side]),
             g if side == 0 else 1 - g,
         )
+    for chunk in rest[EARLY:]:
+        total = total + hot.scatter(chunk, mass)
+    field[...] = plane - (total[:ny] + total[ny:])
+    planes = planes + mix(1)
+    theirs = pl.ds(half, half)
+    size_send[...] = sizes[theirs]
+    sent_back = remote(6, size_send, back, partner)
     sent_back.wait_recv()
     mine = pl.ds(0, half)
     final = jnp.where(hot.here(cells[mine]), sizes[mine], back[...])

time: 32.6 us -> 29.5 us (0.905)
  Pallas kernels: 30.9 us -> 28 us
    pallas_call x1, Pallas kernels: 22.5 us -> 21 us  [local(): pl.pallas_call(run, out_shape=shapes, in_specs=[in_hbm] * 2 + [in_vmem] *...]
    pallas_call x1, Pallas kernels: 7.75 us -> 6.37 us  [local(): pl.pallas_call(meet, out_shape=(shape((ny, nz), F32), shape(both, F32), s...]
where the time goes in v4:
time: 29.5 us; the launch traced here: 29.3 us
  Pallas kernels  28 us (95%)
  between operations  1.29 us (4%)
    pallas_call x1, Pallas kernels, local(): pl.pallas_call(run, out_shape=shapes, in_specs=[in_hbm] * 2 + [in_vmem] *...  21 us
    pallas_call x1, Pallas kernels, local(): pl.pallas_call(meet, out_shape=(shape((ny, nz), F32), shape(both, F32), s...  6.37 us
    pallas_call x1, Pallas kernels, local(): pl.pallas_call(store, out_shape=shapes, in_specs=[anywhere] * 3, out_spec...  0.66 us

profile of v4, /device:TPU:24, one launch (start us, length us, event | category | flops | bytes accessed | tf_op | source)
XLA Modules:
  0.0 29.3 jit_solution(4599270230050296818)
XLA Ops:
  1.3 6.4 %meet.1 = (f32[64,256]{1,0:T(8,128)S(1)}, f32[8,8,128]{2,1,0:T(8,128)S(1)}, f32[8,8,128]{2,1,0:T(8,128)S(1)}, s32[8,8,128]{2,1,0:T(8,128)S(1)}, s32[2,4,512]{2,1...) custom-call(s32[1]{0:T(128)S(6)} %copy.13.live_ref, ...), custom_call_target="tpu_custom_call" | custom-call | tf_op jit(solution)/shard_map/meet/pallas_call | solution.py:593
  7.7 21.0 %run.1 = (f32[1,64,256]{2,1,0:T(8,128)S(1)}, f32[4,8,128]{2,1,0:T(8,128)S(1)}, f32[1,2,2,512]{3,2,1,0:T(2,128)S(1)}) custom-call(s32[1,2]{1,0:T(1,128)} %mcount_hbm.1, s32[1,64,256]{2,1,0:T(8,128)} %inlet_hbm.1, f32[64,256]{1,0:T(8,128)S(1)} %get-tuple-element.20.field_in, f32[8,8,128]{2,1,0:T(8,128)S(1)} %get-tuple-element.21.sizes_in, ...), custom_call_target="tpu_custom_call" | custom-call | tf_op jit(solution)/shard_map/run/pallas_call | solution.py:644
  28.7 0.7 %store.1 = (f32[1,64,256]{2,1,0:T(8,128)}, f32[4,8,128]{2,1,0:T(8,128)}, f32[1,2,2,512]{3,2,1,0:T(2,128)}) custom-call(f32[1,64,256]{2,1,0:T(8,128)S(1)} %get-tuple-element.31.field_ref, f32[4,8,128]{2,1,0:T(8,128)S(1)} %get-tuple-element.32.size_ref, f32[1,2,2,512]{3,2,1,0:T(2,128)S(1)} %get-tuple-element.33.arrive_ref), custom_call_target="tpu_custom_call" | custom-call | tf_op jit(solution)/shard_map/store/pallas_call | solution.py:678

commit v5 on v4

--- a/solution.py
+++ b/solution.py
@@ -17,7 +17,9 @@
 ROWS = 8
 CHUNK = ROWS * LANES
 EARLY = 1
-LAG = 1
+LAG = 2
+BLOCK = 4
+LANE_CHUNKS = 3
 MESH = pl.DeviceIdType.MESH
 F32 = jnp.float32
 BF16 = jnp.bfloat16
@@ -54,6 +56,7 @@
         self.base, self.ny, self.nz = base, ny, nz
         self.shift = nz.bit_length() - 1
         self.chunks = {}
+        self.by_lane = {}
 
     def add(self, first, refs):
         for index in range(refs[0].shape[0]):
@@ -81,9 +84,10 @@
                 return jnp.broadcast_to(row, shape).astype(BF16)
 
             row = slice(j, j + 1)
-            hot_p[at, :, columns] = jnp.where(
-                down_nz == spread(placed[row, :], down_nz.shape), one, none
-            )
+            if chunk not in self.by_lane:
+                hot_p[at, :, columns] = jnp.where(
+                    down_nz == spread(placed[row, :], down_nz.shape), one, none
+                )
             hot_l[at, :, columns] = jnp.where(
                 down_ny == spread(lined[row, :], down_ny.shape), one, none
             )
@@ -95,7 +99,10 @@
         line = (cells - self.base) >> self.shift
         return jnp.logical_and(line >= 0, line < self.ny)
 
-    def gather(self, chunk, pair, local):
+    def gather(self, chunk, table, pair, local):
+        if chunk in self.by_lane:
+            local[chunk] = self.gather_lanes(self.by_lane[chunk]() - self.base, table)
+            return
         hot_p, _, hot_l, at = self.chunks[chunk]
         ny = self.ny
         both = jnp.dot(pair[...], hot_p[at], preferred_element_type=F32)
@@ -103,6 +110,23 @@
         flat = jnp.sum(read, axis=0, keepdims=True)
         for j in range(ROWS):
             local[chunk, pl.ds(j, 1), :] = flat[:, LANES * j : LANES * (j + 1)]
+
+    def gather_lanes(self, cell, table):
+        place = cell & (LANES - 1)
+        row_of = cell >> (LANES.bit_length() - 1)
+        across = self.nz // LANES
+        found = [jnp.zeros((ROWS, LANES), F32) for _ in range(2)]
+        for row in range(self.ny * across):
+            columns = pl.ds(LANES * (row % across), LANES)
+            line = table[pl.ds(row // across, 1), columns]
+            read = jnp.take_along_axis(
+                jnp.broadcast_to(line, (ROWS, LANES)),
+                place,
+                axis=1,
+                mode="promise_in_bounds",
+            )
+            found[row % 2] = jnp.where(row_of == row, read, found[row % 2])
+        return found[0] + found[1]
 
     def scatter(self, chunk, mass):
         _, hot_t, hot_l, at = self.chunks[chunk]
@@ -127,18 +151,30 @@
     mass[chunk, 1] = value - top
 
 
-def deposit(chunks, total, hot, pair, local, mass, weigh):
-    for k in range(len(chunks) + 1):
+def in_turn(hot, chunks):
+    by_lane = [c for c in chunks if c in hot.by_lane]
+    others = [c for c in chunks if c not in hot.by_lane]
+    out = []
+    while by_lane or others:
+        out += others[:1] + by_lane[:1]
+        others, by_lane = others[1:], by_lane[1:]
+    return out
+
+
+def deposit(chunks, total, hot, table, pair, local, mass, weigh):
+    chunks = in_turn(hot, chunks)
+    for k in range(len(chunks) + LAG):
         if k < len(chunks):
-            hot.gather(chunks[k], pair, local)
+            hot.gather(chunks[k], table, pair, local)
             weigh(chunks[k])
-        if k >= 1:
-            total = total + hot.scatter(chunks[k - 1], mass)
+        if k >= LAG:
+            total = total + hot.scatter(chunks[k - LAG], mass)
     return total
 
 
-def split(plane, pair):
+def split(plane, table, pair):
     ny = plane.shape[0]
+    table[...] = plane
     top, rest = pieces(plane, 2)
     pair[pl.ds(0, ny), :] = top
     pair[pl.ds(ny, ny), :] = rest
@@ -165,6 +201,17 @@
             cell.append(ncell[side, sub : sub + 1, columns])
             count.append(ncount[side, sub : sub + 1, columns])
     return jnp.concatenate(cell, axis=0), jnp.concatenate(count, axis=0).astype(F32)
+
+
+def read_by_lane(hot, cells, ncell, ncount):
+    parcel_chunks = cells.shape[0]
+    for chunk in range(parcel_chunks):
+        if chunk % BLOCK >= BLOCK - LANE_CHUNKS:
+            hot.by_lane[chunk] = lambda chunk=chunk: cells[chunk]
+    for sub in range(STEPS * SUBS):
+        hot.by_lane[parcel_chunks + sub] = lambda sub=sub: event_tiles(
+            sub, ncell, ncount
+        )[0]
 
 
 def meet(
@@ -194,6 +241,7 @@
     got_ncell,
     got_ncount,
     got_mrows,
+    table,
     pair,
     local,
     mass,
@@ -261,14 +309,15 @@
 
     hot = Hot(g * (ny * nz), ny, nz)
     hot.add(0, (hot_p, hot_t, hot_l))
+    read_by_lane(hot, cells, ncell, ncount)
     for chunk in range(half):
         hot.build(chunk, cells[chunk])
     for copy in loads[1:]:
         copy.wait()
-    split(field[...], pair)
+    split(field[...], table, pair)
     grow = grower(hot, cells, sizes, weights, local, mass)
     zero = jnp.zeros((2 * ny, nz), F32)
-    total[...] = deposit(list(range(half)), zero, hot, pair, local, mass, grow)
+    total[...] = deposit(list(range(half)), zero, hot, table, pair, local, mass, grow)
 
     theirs = pl.ds(half, half)
     entry[0].wait_recv()
@@ -321,6 +370,7 @@
     late_p,
     late_t,
     late_l,
+    table,
     pair,
     local,
     mass,
@@ -375,6 +425,7 @@
     hot = Hot(g * (ny * nz), ny, nz)
     hot.add(0, (hot_p, hot_t, hot_l))
     hot.add(hot_p.shape[0], (late_p, late_t, late_l))
+    read_by_lane(hot, cells, ncell, ncount)
     sizes[...] = sizes_in[...]
     grow = grower(hot, cells, sizes, weights, local, mass)
 
@@ -389,8 +440,8 @@
         evcount[sub] = event_tiles(sub, ncell, ncount)[1]
 
     def substep(plane, chunks, total):
-        split(plane, pair)
-        total = deposit(chunks, total, hot, pair, local, mass, weigh)
+        split(plane, table, pair)
+        total = deposit(chunks, total, hot, table, pair, local, mass, weigh)
         field[...] = plane - (total[:ny] + total[ny:])
 
     lane = lax.broadcasted_iota(I32, (ny, nz), 1)
@@ -484,23 +535,22 @@
         hot.build(parcel_chunks + sub, event_tiles(sub, ncell, ncount)[0])
     substep(mixed(0, planes), every + [parcel_chunks + 2], zero)
     plane = field[...]
-    split(plane, pair)
+    split(plane, table, pair)
     events = parcel_chunks + 3
     total = zero
-    done = 0
-    for chunk in [events] + every:
-        hot.gather(chunk, pair, local)
+    waiting = []
+    for chunk in in_turn(hot, every + [events]):
+        hot.gather(chunk, table, pair, local)
         weigh(chunk)
-        if chunk < events and chunk >= LAG:
-            total = total + hot.scatter(chunk - LAG, mass)
-            done = chunk - LAG + 1
+        waiting.append(chunk)
+        if len(waiting) > LAG:
+            total = total + hot.scatter(waiting.pop(0), mass)
     for side in range(2):
         at = pl.ds(side * half, half)
         flat = flat_pieces(jnp.where(hot.here(cells[at]), sizes[at], 0.0), 2)
         for j in range(2):
             mig_size[side, j] = pick(side, j, flat)
-    rest = every[done:] + [events]
-    for chunk in rest[:EARLY]:
+    for chunk in waiting[:EARLY]:
         total = total + hot.scatter(chunk, mass)
     for side in range(2):
         send_both(
@@ -509,7 +559,7 @@
             (got_size.at[0, side], got_size.at[1, side]),
             g if side == 0 else 1 - g,
         )
-    for chunk in rest[EARLY:]:
+    for chunk in waiting[EARLY:]:
         total = total + hot.scatter(chunk, mass)
     field[...] = plane - (total[:ny] + total[ny:])
     planes = planes + mix(1)
@@ -615,6 +665,7 @@
             vmem((subs, events), I32),
             vmem((subs, events), I32),
             vmem((2, slots), I32),
+            vmem((ny, nz), F32),
             vmem((2 * ny, nz), BF16),
             vmem((chunks, ROWS, LANES), F32),
             vmem((chunks, 2, ROWS, LANES), F32),
@@ -662,6 +713,7 @@
             vmem((chunks - early, nz, CHUNK), BF16),
             vmem((chunks - early, CHUNK, nz), BF16),
             vmem((chunks - early, ny, CHUNK), BF16),
+            vmem((ny, nz), F32),
             vmem((2 * ny, nz), BF16),
             vmem((chunks, ROWS, LANES), F32),
             vmem((chunks, 2, ROWS, LANES), F32),

time: 29.5 us -> 28 us (0.949)
  Pallas kernels: 28 us -> 26.5 us
    pallas_call x1, Pallas kernels: 21 us -> 20.1 us  [local(): pl.pallas_call(run, out_shape=shapes, in_specs=[in_hbm] * 2 + [in_vmem] *...]
    pallas_call x1, Pallas kernels: 6.37 us -> 5.72 us  [local(): pl.pallas_call(meet, out_shape=(shape((ny, nz), F32), shape(both, F32), s...]
where the time goes in v5:
time: 28 us; the launch traced here: 27.8 us
  Pallas kernels  26.5 us (95%)
  between operations  1.29 us (5%)
    pallas_call x1, Pallas kernels, local(): pl.pallas_call(run, out_shape=shapes, in_specs=[in_hbm] * 2 + [in_vmem] *...  20.1 us
    pallas_call x1, Pallas kernels, local(): pl.pallas_call(meet, out_shape=(shape((ny, nz), F32), shape(both, F32), s...  5.72 us
    pallas_call x1, Pallas kernels, local(): pl.pallas_call(store, out_shape=shapes, in_specs=[anywhere] * 3, out_spec...  0.66 us

profile of v5, /device:TPU:24, one launch (start us, length us, event | category | flops | bytes accessed | tf_op | source)
XLA Modules:
  0.0 27.8 jit_solution(5667856105774825504)
XLA Ops:
  1.3 5.7 %meet.1 = (f32[64,256]{1,0:T(8,128)S(1)}, f32[8,8,128]{2,1,0:T(8,128)S(1)}, f32[8,8,128]{2,1,0:T(8,128)S(1)}, s32[8,8,128]{2,1,0:T(8,128)S(1)}, s32[2,4,512]{2,1...) custom-call(s32[1]{0:T(128)S(6)} %copy.13.live_ref, ...), custom_call_target="tpu_custom_call" | custom-call | tf_op jit(solution)/shard_map/meet/pallas_call | solution.py:643
  7.0 20.1 %run.1 = (f32[1,64,256]{2,1,0:T(8,128)S(1)}, f32[4,8,128]{2,1,0:T(8,128)S(1)}, f32[1,2,2,512]{3,2,1,0:T(2,128)S(1)}) custom-call(s32[1,2]{1,0:T(1,128)} %mcount_hbm.1, s32[1,64,256]{2,1,0:T(8,128)} %inlet_hbm.1, f32[64,256]{1,0:T(8,128)S(1)} %get-tuple-element.20.field_in, f32[8,8,128]{2,1,0:T(8,128)S(1)} %get-tuple-element.21.sizes_in, ...), custom_call_target="tpu_custom_call" | custom-call | tf_op jit(solution)/shard_map/run/pallas_call | solution.py:695
  27.1 0.7 %store.1 = (f32[1,64,256]{2,1,0:T(8,128)}, f32[4,8,128]{2,1,0:T(8,128)}, f32[1,2,2,512]{3,2,1,0:T(2,128)}) custom-call(f32[1,64,256]{2,1,0:T(8,128)S(1)} %get-tuple-element.31.field_ref, f32[4,8,128]{2,1,0:T(8,128)S(1)} %get-tuple-element.32.size_ref, f32[1,2,2,512]{3,2,1,0:T(2,128)S(1)} %get-tuple-element.33.arrive_ref), custom_call_target="tpu_custom_call" | custom-call | tf_op jit(solution)/shard_map/store/pallas_call | solution.py:730
